TPU v7x, 32 devices: a whole 2x2x4 slice. The times are simulated.
32 devices in a mesh: member: 2 (over x), block: 16 (over z, y, core).
Axes of the slice: x: 2, y: 2, z: 4, core: 2. Of those that a mesh axis runs over, the one named last changes fastest.
Arguments:
- grid_in: bfloat16 [32768, 128], P(('member', 'block')), parts along dimension 0, may hold values from -6 to 6
- dest_block: int32 [32768, 1], P(('member', 'block')), parts along dimension 0, may hold values from 0 to 15, as said below
- dest_node: int32 [32768], P(('member', 'block')), parts along dimension 0, may hold values from 0 to 255
- neighbour_mask: int32 [8192, 4], P(('member', 'block')), parts along dimension 0, may hold values 0 or 1
- mesh_embed: bfloat16 [8192, 512], P(('member', 'block')), parts along dimension 0, may hold values from -6 to 6
- w_in: bfloat16 [128, 512], replicated, may hold values from -0.5 to 0.5
- in_bias: bfloat16 [512], replicated, may hold values from -3 to 3
- w_grid: bfloat16 [512, 512], replicated, may hold values from -0.25 to 0.25
- w_enc: bfloat16 [512, 512], replicated, may hold values from -0.25 to 0.25
- attn_gain: bfloat16 [2, 512], replicated, may hold values from 0.099609375 to 1.8984375
- w_query: bfloat16 [2, 512, 512], replicated, may hold values from -0.25 to 0.25
- w_key: bfloat16 [2, 512, 512], replicated, may hold values from -0.25 to 0.25
- w_value: bfloat16 [2, 512, 512], replicated, may hold values from -0.25 to 0.25
- w_out: bfloat16 [2, 512, 512], replicated, may hold values from -0.25 to 0.25
- mlp_gain: bfloat16 [2, 512], replicated, may hold values from 0.099609375 to 1.8984375
- w_up: bfloat16 [2, 512, 512], replicated, may hold values from -0.25 to 0.25
- w_down: bfloat16 [2, 512, 512], replicated, may hold values from -0.25 to 0.25
- dec_gain: bfloat16 [512], replicated, may hold values from 0.099609375 to 1.8984375
- w_dec: bfloat16 [512, 512], replicated, may hold values from -0.25 to 0.25
- w_head: bfloat16 [512, 512], replicated, may hold values from -0.25 to 0.25
- w_final: bfloat16 [512, 128], replicated, may hold values from -0.25 to 0.25
Outputs:
- grid_out: bfloat16 [32768, 128], P(('member', 'block')), parts along dimension 0
There are 2 independent parts, one for each index of `member`. A program takes and returns all parts, laid end to end along the dimension named above; an argument that names none is the same for every part. Nothing has to cross between parts.
Inputs may be any that keep to these rules, and one draw needn't show every extreme that they name: `dest_block`: A grid point of block b maps into one of the mesh blocks b-2, b-1, b, b+1, b+2 (modulo 16); within the 1024 rows of one block exactly 512 name one of these five, and the others name fewer.
All inputs are finite; a program needn't handle non-finite values. No bound on the sum of `neighbour_mask` on one device may be relied on, other than what follows from the above.
Results may differ from a plain program's by a relative error of at most 0.014.
Values may be sent and summed in bfloat16 or wider, within the bound.
No kernel may reach another device: no remote copies, remote signals or barrier semaphores. Data moves between devices by JAX's collectives and lax.ppermute only.
A program may use at most 64 MiB of HBM per device.

v0:
```python
import jax
import jax.numpy as jnp
from jax import lax
from jax.sharding import PartitionSpec as P

HEADS = 8
LAYERS = 2


def shifted(value, axis, steps):
    count = lax.axis_size(axis)
    pairs = [(source, (source + steps) % count) for source in range(count)]
    return lax.ppermute(value, axis, pairs)


def rms_norm(values, gain):
    return (
        values
        * lax.rsqrt(jnp.mean(values * values, axis=-1, keepdims=True) + 1e-06)
        * gain.astype(jnp.float32)
    )


def grid_mlp(rows, w_in, in_bias, w_grid):
    grid_hidden = jax.nn.silu(
        jnp.dot(rows, w_in, preferred_element_type=jnp.float32) + in_bias.astype(jnp.float32)
    ).astype(jnp.bfloat16)
    return jnp.dot(grid_hidden, w_grid, preferred_element_type=jnp.float32).astype(jnp.bfloat16)


def attend(query_rows, key_rows, value_rows, allowed):
    row_count, feature_width = query_rows.shape
    head_dim = feature_width // HEADS
    queries = query_rows.reshape(row_count, HEADS, head_dim).transpose(1, 0, 2)
    keys_near = key_rows.reshape(-1, HEADS, head_dim).transpose(1, 0, 2)
    values_near = value_rows.reshape(-1, HEADS, head_dim).transpose(1, 0, 2)

    def single(operands):
        query_head, key_head, value_head = operands
        scores = lax.dot_general(
            query_head, key_head, (((1,), (1,)), ((), ())), preferred_element_type=jnp.float32
        ) * head_dim ** (-0.5)
        scores = jnp.where(allowed[:, :, None], scores.reshape(row_count, 5, -1), -jnp.inf).reshape(
            row_count, -1
        )
        largest = jnp.max(scores, axis=-1, keepdims=True)
        exponent = jnp.exp(scores - largest)
        softmax_weights = (exponent / jnp.sum(exponent, axis=-1, keepdims=True)).astype(
            jnp.bfloat16
        )
        return jnp.dot(softmax_weights, value_head, preferred_element_type=jnp.float32).astype(
            jnp.bfloat16
        )

    attended = lax.map(single, (queries, keys_near, values_near))
    return attended.transpose(1, 0, 2).reshape(row_count, feature_width)


def nearby_states(normed):
    pieces = []
    for offset in (-2, -1, 0, 1, 2):
        if offset == 0:
            pieces.append(normed)
        else:
            pieces.append(shifted(normed, "block", -offset))
    return jnp.concatenate(pieces, axis=0)


def body(
    grid_in,
    dest_block,
    dest_node,
    neighbour_mask,
    mesh_embed,
    w_in,
    in_bias,
    w_grid,
    w_enc,
    attn_gain,
    w_query,
    w_key,
    w_value,
    w_out,
    mlp_gain,
    w_up,
    w_down,
    dec_gain,
    w_dec,
    w_head,
    w_final,
):
    block_count = lax.axis_size("block")
    my_index = lax.axis_index("block")
    grid_rows = grid_in.shape[0]
    mesh_rows = mesh_embed.shape[0]
    feature_width = w_enc.shape[0]
    capacity = grid_rows // 2
    grid_feat = grid_mlp(grid_in, w_in, in_bias, w_grid)
    destination = dest_block[:, 0]
    relative = (destination - my_index) % block_count
    offset_index = jnp.where(relative > block_count // 2, relative - block_count, relative) + 2
    one_hot = (offset_index[:, None] == jnp.arange(5, dtype=jnp.int32)[None, :]).astype(jnp.int32)
    earlier = jnp.cumsum(one_hot, axis=0) - one_hot
    slot_index = jnp.sum(earlier * one_hot, axis=1)
    placement_index = offset_index * capacity + slot_index
    source_row = (
        jnp.full((5 * capacity,), grid_rows, jnp.int32)
        .at[placement_index]
        .set(jnp.arange(grid_rows, dtype=jnp.int32))
    )
    node_slots = (
        jnp.full((5 * capacity,), -1, jnp.int32)
        .at[placement_index]
        .set(dest_node)
        .reshape(5, capacity)
    )
    padded = jnp.concatenate([grid_feat, jnp.zeros((1, grid_feat.shape[1]), jnp.bfloat16)], axis=0)
    outgoing = padded[source_row].reshape(5, capacity, grid_feat.shape[1])
    received = [None] * 5
    received_nodes = [None] * 5
    received[2] = outgoing[2]
    received_nodes[2] = node_slots[2]
    for offset in (-2, -1, 1, 2):
        got_rows, got_nodes = shifted(
            (outgoing[offset + 2], node_slots[offset + 2]), "block", offset
        )
        received[offset + 2] = got_rows
        received_nodes[offset + 2] = got_nodes
    incoming = jnp.stack(received).reshape(5 * capacity, grid_feat.shape[1])
    arrived = jnp.stack(received_nodes)
    matches = arrived.reshape(-1)[:, None] == jnp.arange(mesh_rows, dtype=jnp.int32)[None, :]
    summed = lax.dot_general(
        matches.astype(jnp.bfloat16),
        incoming,
        (((0,), (0,)), ((), ())),
        preferred_element_type=jnp.float32,
    )
    counts = jnp.sum(matches.astype(jnp.float32), axis=0)
    mean_rows = (summed / jnp.maximum(counts, 1.0)[:, None]).astype(jnp.bfloat16)
    mesh_state = mesh_embed.astype(jnp.float32) + jnp.dot(
        mean_rows, w_enc, preferred_element_type=jnp.float32
    )
    allowed = (
        jnp.concatenate(
            [neighbour_mask[:, :2], jnp.ones((mesh_rows, 1), jnp.int32), neighbour_mask[:, 2:]],
            axis=1,
        )
        > 0
    )
    for layer_index in range(LAYERS):
        normed = rms_norm(mesh_state, attn_gain[layer_index]).astype(jnp.bfloat16)
        query_rows = jnp.dot(
            normed, w_query[layer_index], preferred_element_type=jnp.float32
        ).astype(jnp.bfloat16)
        nearby = nearby_states(normed)
        keys_near = jnp.dot(nearby, w_key[layer_index], preferred_element_type=jnp.float32).astype(
            jnp.bfloat16
        )
        values_near = jnp.dot(
            nearby, w_value[layer_index], preferred_element_type=jnp.float32
        ).astype(jnp.bfloat16)
        attended = attend(query_rows, keys_near, values_near, allowed)
        mesh_state = mesh_state + jnp.dot(
            attended, w_out[layer_index], preferred_element_type=jnp.float32
        )
        normed_second = rms_norm(mesh_state, mlp_gain[layer_index]).astype(jnp.bfloat16)
        up_hidden = jax.nn.silu(
            jnp.dot(normed_second, w_up[layer_index], preferred_element_type=jnp.float32)
        ).astype(jnp.bfloat16)
        mesh_state = mesh_state + jnp.dot(
            up_hidden, w_down[layer_index], preferred_element_type=jnp.float32
        )
    decoded = rms_norm(mesh_state, dec_gain).astype(jnp.bfloat16)
    answer_rows = decoded[jnp.clip(arrived, 0, mesh_rows - 1)]
    returned = [None] * 5
    returned[2] = answer_rows[2]
    for offset in (-2, -1, 1, 2):
        returned[offset + 2] = shifted(answer_rows[offset + 2], "block", -offset)
    gathered = jnp.stack(returned).reshape(-1, feature_width)[placement_index]
    grid_mix = (
        grid_feat.astype(jnp.float32) + jnp.dot(gathered, w_dec, preferred_element_type=jnp.float32)
    ).astype(jnp.bfloat16)
    head_rows = jax.nn.silu(jnp.dot(grid_mix, w_head, preferred_element_type=jnp.float32)).astype(
        jnp.bfloat16
    )
    return jnp.dot(head_rows, w_final, preferred_element_type=jnp.float32).astype(jnp.bfloat16)


def solution(mesh):
    placed = (
        P(("member", "block"), None),
        P(("member", "block"), None),
        P(("member", "block")),
        P(("member", "block"), None),
        P(("member", "block"), None),
        P(),
        P(),
        P(),
        P(),
        P(),
        P(),
        P(),
        P(),
        P(),
        P(),
        P(),
        P(),
        P(),
        P(),
        P(),
        P(),
    )
    return jax.shard_map(
        body, mesh=mesh, in_specs=placed, out_specs=P(("member", "block"), None), check_vma=False
    )
```

profile of v0, /device:TPU:0, one launch (start us, length us, event | category | flops | bytes accessed | tf_op | source)
XLA Modules:
  0.0 260.0 jit_solution(18063617188250358340)
XLA Ops:
  0.8 1.4 reduce-window.6
  3.5 4.5 %scatter_custom_fusion = s32[2560]{0:T(1024)S(1)} fusion(s32[1024]{0:T(1024)S(1)} %bitcast.241, s32[1024]{0:T(1024)} %param.27, s32[]{:T(128)} %constant.61.clone.1), kind=kCustom, calls=%fused_computation.156 | custom fusion | bytes 10752 | tf_op jit(solution)/shard_map/scatter | solution.py:114
  8.0 6.1 %collective-permute-start = (s32[512]{0:T(512)S(1)}, s32[512]{0:T(512)S(1)}, u32[]{:S(2)}, u32[]{:S(2)}) collective-permute-start(s32[512]{0:T(512)S(1)} %get-tuple-element.135), channel_id=1, source_target_pairs={{0,14},{1,15},{2,0},{3,1},{4,2},{5,3},{6,4},{7,5},{8,6},{9,7},{10,... | collective-permute-start | bytes 6152 | tf_op jit(solution)/shard_map/ppermute | solution.py:13
  15.2 4.3 %scatter_custom_fusion.1 = s32[2560]{0:T(1024)S(1)} fusion(s32[1024]{0:T(1024)S(1)} %bitcast.242, s32[1024]{0:T(1024)S(1)} %iota.15, s32[]{:T(128)} %constant.98.clone.1), kind=kCustom, calls=%fused_computation.154 | custom fusion | bytes 10244 | tf_op jit(solution)/shard_map/scatter | solution.py:109
  21.0 2.1 convolution_convert_fusion.6
  23.5 8.2 %gather_fusion = bf16[2560,512]{1,0:T(8,128)(2,1)} fusion(bf16[1025,512]{1,0:T(8,128)(2,1)S(1)} %concatenate.19, s32[3072]{0:T(1024)S(1)} %get-tuple-element.153), kind=kCustom, calls=%fused_computation | custom fusion | bytes 5253120 | tf_op jit(solution)/shard_map/gather | solution.py:118
  31.7 2.7 %fusion.97 = (bf16[512,512]{1,0:T(8,128)(2,1)S(1)}, bf16[512,512]{1,0:T(8,128)(2,1)}, bf16[512,512]{1,0:T(8,128)(2,1)}, bf16[512,512]{1,0:T(8,128)(2,1)}) fusion(bf16[2560,512]{1,0:T(8,128)(2,1)} %gather_fusion), kind=kLoop, calls=%fused_computation.177 | loop fusion | bytes 4194304 | tf_op jit(solution)/shard_map/slice | solution.py:125
  34.4 4.1 %collective-permute-start.4 = (bf16[512,512]{1,0:T(8,128)(2,1)}, bf16[512,512]{1,0:T(8,128)(2,1)S(1)}, u32[]{:S(2)}, u32[]{:S(2)}) collective-permute-start(bf16[512,512]{1,0:T(8,128)(2,1)} %get-tuple-element.130), channel_id=1, source_target_pairs={{0,14},{1,15},{2,0},{3,1},{4,2},{5,3},{6,4},{7,5},{8,6},{9,7},{10,... | collective-permute-start | bytes 1572872 | tf_op jit(solution)/shard_map/ppermute | solution.py:13
  41.7 23.8 %collective-permute-done.4 = bf16[512,512]{1,0:T(8,128)(2,1)S(1)} collective-permute-done((bf16[512,512]{1,0:T(8,128)(2,1)}, bf16[512,512]{1,0:T(8,128)(2,1)S(1)}, u32[]{:S(2)}, u32[]{:S(2)}) %collective-permute-start.4) | collective-permute-done | bytes 524320 | tf_op jit(solution)/shard_map/ppermute | solution.py:13
  66.8 1.5 copy-done.6
  68.3 3.4 %multiply_reduce_fusion.4 = (f32[256]{0:T(256)S(1)}, f32[256,512]{1,0:T(8,128)S(1)}) fusion(bf16[512,512]{1,0:T(8,128)(2,1)S(1)} %copy-done.14, bf16[2560,512]{1,0:T(8,128)(2,1)} %bitcast.231, s32[2560]{0:T(1024)S(1)} %eq.50, f32[256]{0:T(256)S(1)} %broadcast_maximum_fusion, bf16[256,512]{1,0:T(8,128)(2,1)} %param.29), kind=kOutput, calls=%fused_computation.111 | convolution fusion | flops 806747904 | bytes 3944448 | tf_op jit(solution)/shard_map/dot_general | solution.py:140
  71.9 5.2 %collective-permute-start.8 = (bf16[256,512]{1,0:T(8,128)(2,1)S(1)}, bf16[256,512]{1,0:T(8,128)(2,1)S(1)}, u32[]{:S(2)}, u32[]{:S(2)}) collective-permute-start(bf16[256,512]{1,0:T(8,128)(2,1)S(1)} %multiply_convert_fusion.12), channel_id=1, source_target_pairs={{0,2},{1,3},{2,4},{3,5},{4,6},{5,7},{6,8},{7,9},{8,10},{9,11},{10,... | collective-permute-start | bytes 786440 | tf_op jit(solution)/shard_map/ppermute | solution.py:13
  77.4 4.3 %collective-permute-start.10 = (bf16[256,512]{1,0:T(8,128)(2,1)S(1)}, bf16[256,512]{1,0:T(8,128)(2,1)S(1)}, u32[]{:S(2)}, u32[]{:S(2)}) collective-permute-start(bf16[256,512]{1,0:T(8,128)(2,1)S(1)} %multiply_convert_fusion.12), channel_id=1, source_target_pairs={{0,15},{1,0},{2,1},{3,2},{4,3},{5,4},{6,5},{7,6},{8,7},{9,8},{10,9... | collective-permute-start | bytes 786440 | tf_op jit(solution)/shard_map/ppermute | solution.py:13
  81.6 1.3 collective-permute-start.11
  82.9 1.3 convolution_convert_fusion.9
  85.1 7.1 %collective-permute-done.8 = bf16[256,512]{1,0:T(8,128)(2,1)S(1)} collective-permute-done((bf16[256,512]{1,0:T(8,128)(2,1)S(1)}, bf16[256,512]{1,0:T(8,128)(2,1)S(1)}, u32[]{:S(2)}, u32[]{:S(2)}) %collective-permute-start.8) | collective-permute-done | bytes 262176 | tf_op jit(solution)/shard_map/ppermute | solution.py:13
  92.4 4.9 %collective-permute-done.11 = bf16[256,512]{1,0:T(8,128)(2,1)S(1)} collective-permute-done((bf16[256,512]{1,0:T(8,128)(2,1)S(1)}, bf16[256,512]{1,0:T(8,128)(2,1)S(1)}, u32[]{:S(2)}, u32[]{:S(2)}) %collective-permute-start.11) | collective-permute-done | bytes 262176 | tf_op jit(solution)/shard_map/ppermute | solution.py:13
  97.4 2.0 convolution_convert_fusion.5
  99.4 3.2 %copy.43 = bf16[1280,8,64]{2,0,1:T(8,128)(2,1)S(1)} copy(bf16[1280,8,64]{0,2,1:T(8,128)(2,1)} %bitcast.226) | data formatting | bytes 2621440 | tf_op jit(solution)/shard_map/reshape | solution.py:35
  102.6 3.4 %convolution_convert_fusion.4 = bf16[1280,512]{0,1:T(8,128)(2,1)} fusion(bf16[1280,512]{1,0:T(8,128)(2,1)} %copy-done.7, bf16[2,512,512]{2,1,0:T(8,128)(2,1)} %param.37), kind=kOutput, calls=%fused_computation.39 | convolution fusion | flops 671744000 | bytes 3145728 | tf_op jit(solution)/shard_map/dot_general | solution.py:159
  106.0 3.7 %copy.44 = bf16[1280,8,64]{2,0,1:T(8,128)(2,1)} copy(bf16[1280,8,64]{0,2,1:T(8,128)(2,1)} %bitcast.225) | data formatting | bytes 2621440 | tf_op jit(solution)/shard_map/reshape | solution.py:36
  109.8 28.6 %while.20 = (s32[]{:T(128)}, bf16[8,256,64]{1,2,0:T(8,128)(2,1)S(1)}, pred[256,5]{0,1:T(8,128)(4,1)S(1)}, bf16[8,256,64]{1,2,0:T(8,128)(2,1)}, bf16[8,1280,64]{2...) while((s32[]{:T(128)}, bf16[8,256,64]{1,2,0:T(8,128)(2,1)S(1)}, ...), condition=%wide.region_10.11_spmd, body=%wide.region_7.10_spmd.sunk | while | flops 86523392 | bytes 5972301 | solution.py:55
  110.3 1.3 fusion.131
  111.9 1.4 fusion.133
  115.5 1.4 fusion.133
  119.0 1.4 fusion.133
  121.0 1.3 fusion.131
  122.6 1.4 fusion.133
  126.2 1.4 fusion.133
  129.8 1.4 fusion.133
  133.3 1.4 fusion.133
  136.9 1.4 fusion.133
  138.4 1.6 multiply_reduce_fusion.3
  140.0 1.9 multiply_reduce_fusion.2
  142.2 4.4 %collective-permute-start.14 = (bf16[256,512]{1,0:T(8,128)(2,1)S(1)}, bf16[256,512]{1,0:T(8,128)(2,1)S(1)}, u32[]{:S(2)}, u32[]{:S(2)}) collective-permute-start(bf16[256,512]{1,0:T(8,128)(2,1)S(1)} %multiply_convert_fusion.7), channel_id=1, source_target_pairs={{0,15},{1,0},{2,1},{3,2},{4,3},{5,4},{6,5},{7,6},{8,7},{9,8},{10,9... | collective-permute-start | bytes 786440 | tf_op jit(solution)/shard_map/ppermute | solution.py:13
  146.6 1.9 collective-permute-start.15
  148.6 1.3 convolution_convert_fusion.8
  150.8 5.9 %collective-permute-done.12 = bf16[256,512]{1,0:T(8,128)(2,1)S(1)} collective-permute-done((bf16[256,512]{1,0:T(8,128)(2,1)S(1)}, bf16[256,512]{1,0:T(8,128)(2,1)S(1)}, u32[]{:S(2)}, u32[]{:S(2)}) %collective-permute-start.12) | collective-permute-done | bytes 262176 | tf_op jit(solution)/shard_map/ppermute | solution.py:13
  156.9 4.8 %collective-permute-done.15 = bf16[256,512]{1,0:T(8,128)(2,1)S(1)} collective-permute-done((bf16[256,512]{1,0:T(8,128)(2,1)S(1)}, bf16[256,512]{1,0:T(8,128)(2,1)S(1)}, u32[]{:S(2)}, u32[]{:S(2)}) %collective-permute-start.15) | collective-permute-done | bytes 262176 | tf_op jit(solution)/shard_map/ppermute | solution.py:13
  161.8 2.0 convolution_convert_fusion.3
  163.8 2.0 convolution_convert_fusion.2
  165.8 3.2 %copy.47 = bf16[1280,8,64]{2,0,1:T(8,128)(2,1)S(1)} copy(bf16[1280,8,64]{0,2,1:T(8,128)(2,1)} %bitcast.224) | data formatting | bytes 2621440 | tf_op jit(solution)/shard_map/reshape | solution.py:35
  169.0 3.8 %copy.48 = bf16[1280,8,64]{2,0,1:T(8,128)(2,1)} copy(bf16[1280,8,64]{0,2,1:T(8,128)(2,1)} %bitcast.223) | data formatting | bytes 2621440 | tf_op jit(solution)/shard_map/reshape | solution.py:36
  172.8 28.6 %while.21 = (s32[]{:T(128)}, bf16[8,256,64]{1,2,0:T(8,128)(2,1)S(1)}, pred[256,5]{0,1:T(8,128)(4,1)S(1)}, bf16[8,256,64]{1,2,0:T(8,128)(2,1)}, bf16[8,1280,64]{2...) while((s32[]{:T(128)}, bf16[8,256,64]{1,2,0:T(8,128)(2,1)S(1)}, ...), condition=%wide.region_16.17_spmd, body=%wide.region_13.16_spmd.sunk | while | flops 86523392 | bytes 5972301 | solution.py:55
  174.9 1.4 fusion.137
  178.5 1.4 fusion.137
  180.5 1.3 fusion.135
  182.1 1.4 fusion.137
  184.0 1.3 fusion.135
  185.6 1.4 fusion.137
  189.2 1.4 fusion.137
  192.8 1.4 fusion.137
  196.4 1.4 fusion.137
  199.9 1.4 fusion.137
  201.4 1.6 multiply_reduce_fusion.1
  203.0 1.9 multiply_reduce_fusion
  205.0 7.7 %gather_fusion.1 = bf16[2560,512]{1,0:T(8,128)(2,1)S(1)} fusion(bf16[256,512]{1,0:T(8,128)(2,1)S(1)} %multiply_convert_fusion.2, s32[3072]{0:T(1024)S(1)} %get-tuple-element.152), kind=kCustom, calls=%fused_computation.1 | custom fusion | bytes 5253120 | tf_op jit(solution)/shard_map/gather | solution.py:174
  212.9 1.4 copy-done.1
  214.2 4.4 %collective-permute-start.18 = (bf16[512,512]{1,0:T(8,128)(2,1)S(1)}, bf16[512,512]{1,0:T(8,128)(2,1)S(1)}, u32[]{:S(2)}, u32[]{:S(2)}) collective-permute-start(bf16[512,512]{1,0:T(8,128)(2,1)S(1)} %get-tuple-element.124), channel_id=1, source_target_pairs={{0,15},{1,0},{2,1},{3,2},{4,3},{5,4},{6,5},{7,6},{8,7},{9,8},{10,9... | collective-permute-start | bytes 1572872 | tf_op jit(solution)/shard_map/ppermute | solution.py:13
  218.7 2.0 collective-permute-start.19
  220.7 22.7 %collective-permute-done.16 = bf16[512,512]{1,0:T(8,128)(2,1)S(1)} collective-permute-done((bf16[512,512]{1,0:T(8,128)(2,1)S(1)}, bf16[512,512]{1,0:T(8,128)(2,1)S(1)}, u32[]{:S(2)}, u32[]{:S(2)}) %collective-permute-start.16) | collective-permute-done | bytes 524320 | tf_op jit(solution)/shard_map/ppermute | solution.py:13
  244.6 5.7 %collective-permute-done.19 = bf16[512,512]{1,0:T(8,128)(2,1)S(1)} collective-permute-done((bf16[512,512]{1,0:T(8,128)(2,1)S(1)}, bf16[512,512]{1,0:T(8,128)(2,1)S(1)}, u32[]{:S(2)}, u32[]{:S(2)}) %collective-permute-start.19) | collective-permute-done | bytes 524320 | tf_op jit(solution)/shard_map/ppermute | solution.py:13
  250.3 5.1 %gather_fusion.2 = bf16[1024,512]{1,0:T(8,128)(2,1)} fusion(bf16[2560,512]{1,0:T(8,128)(2,1)S(1)} %bitcast.218, s32[1024]{0:T(1024)S(1)} %broadcast_clamp_fusion), kind=kCustom, calls=%fused_computation.2 | custom fusion | bytes 2101248 | tf_op jit(solution)/shard_map/gather | solution.py:179
  255.4 3.4 %multiply_convert_fusion = bf16[1024,512]{1,0:T(8,128)(2,1)S(1)} fusion(bf16[512,512]{1,0:T(8,128)(2,1)} %param.44, bf16[1024,512]{1,0:T(8,128)(2,1)} %copy-done.4, bf16[1024,512]{1,0:T(8,128)(2,1)} %gather_fusion.2, bf16[512,512]{1,0:T(8,128)(2,1)} %param.43), kind=kOutput, calls=%fused_computation.44 | convolution fusion | flops 1077936128 | bytes 4194304 | tf_op jit(solution)/shard_map/dot_general | solution.py:183
  (177 shorter events, 43.3 us)
Async XLA Ops:
  0.0 21.0 %copy-start = (bf16[512,512]{1,0:T(8,128)(2,1)S(1)}, bf16[512,512]{1,0:T(8,128)(2,1)}, u32[]{:S(2)}) copy-start(bf16[512,512]{1,0:T(8,128)(2,1)} %param.32) | copy-start | bytes 1572868
  8.0 15.4 %collective-permute-start = (s32[512]{0:T(512)S(1)}, s32[512]{0:T(512)S(1)}, u32[]{:S(2)}, u32[]{:S(2)}) collective-permute-start(s32[512]{0:T(512)S(1)} %get-tuple-element.135), channel_id=1, source_target_pairs={{0,14},{1,15},{2,0},{3,1},{4,2},{5,3},{6,4},{7,5},{8,6},{9,7},{10,... | collective-permute-start | bytes 6152 | tf_op jit(solution)/shard_map/ppermute | solution.py:13
  14.0 9.3 %collective-permute-start.1 = (s32[512]{0:T(512)S(1)}, s32[512]{0:T(512)S(1)}, u32[]{:S(2)}, u32[]{:S(2)}) collective-permute-start(s32[512]{0:T(512)S(1)} %get-tuple-element.134), channel_id=1, source_target_pairs={{0,15},{1,0},{2,1},{3,2},{4,3},{5,4},{6,5},{7,6},{8,7},{9,8},{10,9... | collective-permute-start | bytes 6152 | tf_op jit(solution)/shard_map/ppermute | solution.py:13
  14.1 9.3 %collective-permute-start.2 = (s32[512]{0:T(512)S(1)}, s32[512]{0:T(512)S(1)}, u32[]{:S(2)}, u32[]{:S(2)}) collective-permute-start(s32[512]{0:T(512)S(1)} %get-tuple-element.132), channel_id=1, source_target_pairs={{0,1},{1,2},{2,3},{3,4},{4,5},{5,6},{6,7},{7,8},{8,9},{9,10},{10,1... | collective-permute-start | bytes 6152 | tf_op jit(solution)/shard_map/ppermute | solution.py:13
  14.6 8.9 %collective-permute-start.3 = (s32[512]{0:T(512)S(1)}, s32[512]{0:T(512)S(1)}, u32[]{:S(2)}, u32[]{:S(2)}) collective-permute-start(s32[512]{0:T(512)S(1)} %get-tuple-element.131), channel_id=1, source_target_pairs={{0,2},{1,3},{2,4},{3,5},{4,6},{5,7},{6,8},{7,9},{8,10},{9,11},{10,... | collective-permute-start | bytes 6152 | tf_op jit(solution)/shard_map/ppermute | solution.py:13
  21.0 2.1 copy-start.8
  23.2 8.6 %copy-start.4 = (bf16[1024,512]{1,0:T(8,128)(2,1)}, bf16[1024,512]{1,0:T(8,128)(2,1)S(1)}, u32[]{:S(2)}) copy-start(bf16[1024,512]{1,0:T(8,128)(2,1)S(1)} %convolution_convert_fusion.6) | copy-start | bytes 3145732
  31.7 6.8 %copy-start.9 = (bf16[2,512]{1,0:T(2,128)(2,1)S(1)}, bf16[2,512]{1,0:T(2,128)(2,1)}, u32[]{:S(2)}) copy-start(bf16[2,512]{1,0:T(2,128)(2,1)} %param.39) | copy-start | bytes 6148
  34.4 31.0 %collective-permute-start.4 = (bf16[512,512]{1,0:T(8,128)(2,1)}, bf16[512,512]{1,0:T(8,128)(2,1)S(1)}, u32[]{:S(2)}, u32[]{:S(2)}) collective-permute-start(bf16[512,512]{1,0:T(8,128)(2,1)} %get-tuple-element.130), channel_id=1, source_target_pairs={{0,14},{1,15},{2,0},{3,1},{4,2},{5,3},{6,4},{7,5},{8,6},{9,7},{10,... | collective-permute-start | bytes 1572872 | tf_op jit(solution)/shard_map/ppermute | solution.py:13
  38.5 27.0 %collective-permute-start.5 = (bf16[512,512]{1,0:T(8,128)(2,1)}, bf16[512,512]{1,0:T(8,128)(2,1)S(1)}, u32[]{:S(2)}, u32[]{:S(2)}) collective-permute-start(bf16[512,512]{1,0:T(8,128)(2,1)} %get-tuple-element.129), channel_id=1, source_target_pairs={{0,15},{1,0},{2,1},{3,2},{4,3},{5,4},{6,5},{7,6},{8,7},{9,8},{10,9... | collective-permute-start | bytes 1572872 | tf_op jit(solution)/shard_map/ppermute | solution.py:13
  39.2 27.4 %collective-permute-start.6 = (bf16[512,512]{1,0:T(8,128)(2,1)}, bf16[512,512]{1,0:T(8,128)(2,1)S(1)}, u32[]{:S(2)}, u32[]{:S(2)}) collective-permute-start(bf16[512,512]{1,0:T(8,128)(2,1)} %get-tuple-element.128), channel_id=1, source_target_pairs={{0,1},{1,2},{2,3},{3,4},{4,5},{5,6},{6,7},{7,8},{8,9},{9,10},{10,1... | collective-permute-start | bytes 1572872 | tf_op jit(solution)/shard_map/ppermute | solution.py:13
  39.3 27.5 %collective-permute-start.7 = (bf16[512,512]{1,0:T(8,128)(2,1)S(1)}, bf16[512,512]{1,0:T(8,128)(2,1)S(1)}, u32[]{:S(2)}, u32[]{:S(2)}) collective-permute-start(bf16[512,512]{1,0:T(8,128)(2,1)S(1)} %get-tuple-element.127), channel_id=1, source_target_pairs={{0,2},{1,3},{2,4},{3,5},{4,6},{5,7},{6,8},{7,9},{8,10},{9,11},{10,... | collective-permute-start | bytes 1572872 | tf_op jit(solution)/shard_map/ppermute | solution.py:13
  65.5 2.8 %copy-start.14 = (bf16[512,512]{1,0:T(8,128)(2,1)S(1)}, bf16[512,512]{1,0:T(8,128)(2,1)}, u32[]{:S(2)}) copy-start(bf16[512,512]{1,0:T(8,128)(2,1)} %param.33) | copy-start | bytes 1572868
  66.8 1.5 copy-start.6
  71.8 20.7 %copy-start.2 = (f32[256,512]{1,0:T(8,128)}, f32[256,512]{1,0:T(8,128)S(1)}, u32[]{:S(2)}) copy-start(f32[256,512]{1,0:T(8,128)S(1)} %get-tuple-element.143) | copy-start | bytes 1572868
  71.9 20.3 %collective-permute-start.8 = (bf16[256,512]{1,0:T(8,128)(2,1)S(1)}, bf16[256,512]{1,0:T(8,128)(2,1)S(1)}, u32[]{:S(2)}, u32[]{:S(2)}) collective-permute-start(bf16[256,512]{1,0:T(8,128)(2,1)S(1)} %multiply_convert_fusion.12), channel_id=1, source_target_pairs={{0,2},{1,3},{2,4},{3,5},{4,6},{5,7},{6,8},{7,9},{8,10},{9,11},{10,... | collective-permute-start | bytes 786440 | tf_op jit(solution)/shard_map/ppermute | solution.py:13
  77.2 15.1 %collective-permute-start.9 = (bf16[256,512]{1,0:T(8,128)(2,1)S(1)}, bf16[256,512]{1,0:T(8,128)(2,1)S(1)}, u32[]{:S(2)}, u32[]{:S(2)}) collective-permute-start(bf16[256,512]{1,0:T(8,128)(2,1)S(1)} %multiply_convert_fusion.12), channel_id=1, source_target_pairs={{0,1},{1,2},{2,3},{3,4},{4,5},{5,6},{6,7},{7,8},{8,9},{9,10},{10,1... | collective-permute-start | bytes 786440 | tf_op jit(solution)/shard_map/ppermute | solution.py:13
  77.4 15.1 %collective-permute-start.10 = (bf16[256,512]{1,0:T(8,128)(2,1)S(1)}, bf16[256,512]{1,0:T(8,128)(2,1)S(1)}, u32[]{:S(2)}, u32[]{:S(2)}) collective-permute-start(bf16[256,512]{1,0:T(8,128)(2,1)S(1)} %multiply_convert_fusion.12), channel_id=1, source_target_pairs={{0,15},{1,0},{2,1},{3,2},{4,3},{5,4},{6,5},{7,6},{8,7},{9,8},{10,9... | collective-permute-start | bytes 786440 | tf_op jit(solution)/shard_map/ppermute | solution.py:13
  81.6 15.7 %collective-permute-start.11 = (bf16[256,512]{1,0:T(8,128)(2,1)S(1)}, bf16[256,512]{1,0:T(8,128)(2,1)S(1)}, u32[]{:S(2)}, u32[]{:S(2)}) collective-permute-start(bf16[256,512]{1,0:T(8,128)(2,1)S(1)} %multiply_convert_fusion.12), channel_id=1, source_target_pairs={{0,14},{1,15},{2,0},{3,1},{4,2},{5,3},{6,4},{7,5},{8,6},{9,7},{10,... | collective-permute-start | bytes 786440 | tf_op jit(solution)/shard_map/ppermute | solution.py:13
  85.1 12.2 %copy-start.11 = (bf16[2,512,512]{2,1,0:T(8,128)(2,1)S(1)}, bf16[2,512,512]{2,1,0:T(8,128)(2,1)}, u32[]{:S(2)}) copy-start(bf16[2,512,512]{2,1,0:T(8,128)(2,1)} %param.36) | copy-start | bytes 3145732
  97.3 2.0 copy-start.7
  140.0 2.1 copy-start.10
  141.9 15.0 %copy-start.3 = (f32[256,512]{1,0:T(8,128)}, f32[256,512]{1,0:T(8,128)S(1)}, u32[]{:S(2)}) copy-start(f32[256,512]{1,0:T(8,128)S(1)} %get-tuple-element.147) | copy-start | bytes 1572868
  142.0 14.7 %collective-permute-start.12 = (bf16[256,512]{1,0:T(8,128)(2,1)S(1)}, bf16[256,512]{1,0:T(8,128)(2,1)S(1)}, u32[]{:S(2)}, u32[]{:S(2)}) collective-permute-start(bf16[256,512]{1,0:T(8,128)(2,1)S(1)} %multiply_convert_fusion.7), channel_id=1, source_target_pairs={{0,2},{1,3},{2,4},{3,5},{4,6},{5,7},{6,8},{7,9},{8,10},{9,11},{10,... | collective-permute-start | bytes 786440 | tf_op jit(solution)/shard_map/ppermute | solution.py:13
  142.1 14.6 %collective-permute-start.13 = (bf16[256,512]{1,0:T(8,128)(2,1)S(1)}, bf16[256,512]{1,0:T(8,128)(2,1)S(1)}, u32[]{:S(2)}, u32[]{:S(2)}) collective-permute-start(bf16[256,512]{1,0:T(8,128)(2,1)S(1)} %multiply_convert_fusion.7), channel_id=1, source_target_pairs={{0,1},{1,2},{2,3},{3,4},{4,5},{5,6},{6,7},{7,8},{8,9},{9,10},{10,1... | collective-permute-start | bytes 786440 | tf_op jit(solution)/shard_map/ppermute | solution.py:13
  142.2 14.7 %collective-permute-start.14 = (bf16[256,512]{1,0:T(8,128)(2,1)S(1)}, bf16[256,512]{1,0:T(8,128)(2,1)S(1)}, u32[]{:S(2)}, u32[]{:S(2)}) collective-permute-start(bf16[256,512]{1,0:T(8,128)(2,1)S(1)} %multiply_convert_fusion.7), channel_id=1, source_target_pairs={{0,15},{1,0},{2,1},{3,2},{4,3},{5,4},{6,5},{7,6},{8,7},{9,8},{10,9... | collective-permute-start | bytes 786440 | tf_op jit(solution)/shard_map/ppermute | solution.py:13
  146.6 15.2 %collective-permute-start.15 = (bf16[256,512]{1,0:T(8,128)(2,1)S(1)}, bf16[256,512]{1,0:T(8,128)(2,1)S(1)}, u32[]{:S(2)}, u32[]{:S(2)}) collective-permute-start(bf16[256,512]{1,0:T(8,128)(2,1)S(1)} %multiply_convert_fusion.7), channel_id=1, source_target_pairs={{0,14},{1,15},{2,0},{3,1},{4,2},{5,3},{6,4},{7,5},{8,6},{9,7},{10,... | collective-permute-start | bytes 786440 | tf_op jit(solution)/shard_map/ppermute | solution.py:13
  150.8 11.0 %copy-start.12 = (bf16[2,512,512]{2,1,0:T(8,128)(2,1)S(1)}, bf16[2,512,512]{2,1,0:T(8,128)(2,1)}, u32[]{:S(2)}) copy-start(bf16[2,512,512]{2,1,0:T(8,128)(2,1)} %param.36) | copy-start | bytes 3145732
  156.9 6.9 %copy-start.13 = (bf16[2,512,512]{2,1,0:T(8,128)(2,1)S(1)}, bf16[2,512,512]{2,1,0:T(8,128)(2,1)}, u32[]{:S(2)}) copy-start(bf16[2,512,512]{2,1,0:T(8,128)(2,1)} %param.37) | copy-start | bytes 3145732
  212.7 1.5 copy-start.1
  214.2 29.2 %collective-permute-start.16 = (bf16[512,512]{1,0:T(8,128)(2,1)S(1)}, bf16[512,512]{1,0:T(8,128)(2,1)S(1)}, u32[]{:S(2)}, u32[]{:S(2)}) collective-permute-start(bf16[512,512]{1,0:T(8,128)(2,1)S(1)} %get-tuple-element.126), channel_id=1, source_target_pairs={{0,2},{1,3},{2,4},{3,5},{4,6},{5,7},{6,8},{7,9},{8,10},{9,11},{10,... | collective-permute-start | bytes 1572872 | tf_op jit(solution)/shard_map/ppermute | solution.py:13
  214.2 29.2 %collective-permute-start.17 = (bf16[512,512]{1,0:T(8,128)(2,1)S(1)}, bf16[512,512]{1,0:T(8,128)(2,1)S(1)}, u32[]{:S(2)}, u32[]{:S(2)}) collective-permute-start(bf16[512,512]{1,0:T(8,128)(2,1)S(1)} %get-tuple-element.125), channel_id=1, source_target_pairs={{0,1},{1,2},{2,3},{3,4},{4,5},{5,6},{6,7},{7,8},{8,9},{9,10},{10,1... | collective-permute-start | bytes 1572872 | tf_op jit(solution)/shard_map/ppermute | solution.py:13
  214.2 30.3 %collective-permute-start.18 = (bf16[512,512]{1,0:T(8,128)(2,1)S(1)}, bf16[512,512]{1,0:T(8,128)(2,1)S(1)}, u32[]{:S(2)}, u32[]{:S(2)}) collective-permute-start(bf16[512,512]{1,0:T(8,128)(2,1)S(1)} %get-tuple-element.124), channel_id=1, source_target_pairs={{0,15},{1,0},{2,1},{3,2},{4,3},{5,4},{6,5},{7,6},{8,7},{9,8},{10,9... | collective-permute-start | bytes 1572872 | tf_op jit(solution)/shard_map/ppermute | solution.py:13
  218.7 31.6 %collective-permute-start.19 = (bf16[512,512]{1,0:T(8,128)(2,1)S(1)}, bf16[512,512]{1,0:T(8,128)(2,1)S(1)}, u32[]{:S(2)}, u32[]{:S(2)}) collective-permute-start(bf16[512,512]{1,0:T(8,128)(2,1)S(1)} %get-tuple-element.123), channel_id=1, source_target_pairs={{0,14},{1,15},{2,0},{3,1},{4,2},{5,3},{6,4},{7,5},{8,6},{9,7},{10,... | collective-permute-start | bytes 1572872 | tf_op jit(solution)/shard_map/ppermute | solution.py:13
  255.4 3.4 %copy-start.5 = (bf16[512,128]{1,0:T(8,128)(2,1)S(1)}, bf16[512,128]{1,0:T(8,128)(2,1)}, u32[]{:S(2)}) copy-start(bf16[512,128]{1,0:T(8,128)(2,1)} %param.45) | copy-start | bytes 393220
where the time goes:
time: 262 us; the launch traced here: 260 us
  waiting for transfers between devices  74.9 us (29%)
  matrix products  72.2 us (28%)
  local copies, waits for them, and re-layouts  63.1 us (24%)
  starting transfers between devices  37.2 us (14%)
  other arithmetic  11.3 us (4%)
    ppermute x20, waiting for transfers between devices, shifted(): return lax.ppermute(value, axis, pairs)  74.9 us
    ppermute x20, starting transfers between devices, shifted(): return lax.ppermute(value, axis, pairs)  37.2 us
    dot_general x16, matrix products, single(): jnp.dot(softmax_weights, value_head, preferred_element_type=jnp.float32)  23 us
    dot_general x16, matrix products, single(): lax.dot_general(query_head, key_head, (((1,), (1,)), ((), ())), preferred...  20 us
    gather x1, local copies, waits for them, and re-layouts, body(): outgoing = padded[source_row].reshape(5, capacity, grid_feat.shape[1])  8.2 us
    broadcast_in_dim x32, local copies, waits for them, and re-layouts, single(): jnp.where(allowed[:, :, None], scores.reshape(row_count, 5, -1), -jnp.inf)  8.05 us
    gather x1, local copies, waits for them, and re-layouts, body(): answer_rows = decoded[jnp.clip(arrived, 0, mesh_rows - 1)]  7.66 us
    reshape x2, local copies, waits for them, and re-layouts, attend(): values_near = value_rows.reshape(-1, HEADS, head_dim).transpose(1, 0, 2)  7.5 us
  transfers between devices with their start and end apart: 20, of which 7 were waited for; matrix products, arithmetic and copies ran while one was open for 6% of the time, Pallas kernels for 0%

commit v1 on v0

v1 whole, which is shorter than its diff:
```python
import functools

import jax
import jax.numpy as jnp
from jax import lax
from jax.experimental import pallas as pl
from jax.experimental.pallas import tpu as pltpu
from jax.sharding import PartitionSpec as P

HEADS = 8
LAYERS = 2
LANES = 128
BF16 = jnp.bfloat16
F32 = jnp.float32
LOG2E = 1.4426950408889634
FAR = 1e30


OFFSETS = {"own": 0, "pair": 1, "near": -1, "wide": 2, "far": -2}


def send(value, step_even, step_odd):
    count = lax.axis_size("block")
    pairs = [
        (source, (source + (step_even if source % 2 == 0 else step_odd)) % count)
        for source in range(count)
    ]
    return lax.ppermute(value, "block", pairs)


def spread(value):
    near = send(value, -1, 1)
    far = send(value, 2, -2)
    pair = send(value, 1, -1)
    wide = send(near, 1, -1)
    return pair, near, wide, far


def dot(left, right):
    return lax.dot_general(left, right, (((1,), (0,)), ((), ())), preferred_element_type=F32)


def dot_t(left, right):
    return lax.dot_general(left, right, (((1,), (1,)), ((), ())), preferred_element_type=F32)


def silu(values):
    half = 0.5 * values
    return half * (jnp.tanh(half) + 1.0)


def rms(values, gain):
    mean = jnp.mean(values * values, axis=-1, keepdims=True)
    return values * lax.rsqrt(mean + 1e-06) * gain


def codes(packed_ref, grid_rows, sign, offset):
    id_rows = grid_rows // LANES
    node = packed_ref[pl.ds(grid_rows, id_rows), :].astype(F32)
    step = packed_ref[pl.ds(grid_rows + id_rows, id_rows), :].astype(F32) * sign
    return jnp.where(step == float(offset), node, -1.0)


def gather_sums(packed_ref, grid_rows, sign, offset, w_in, bias, total, count):
    mesh_rows = total.shape[0]
    hidden = silu(dot(packed_ref[pl.ds(0, grid_rows), :], w_in) + bias).astype(BF16)
    code = codes(packed_ref, grid_rows, sign, -offset).astype(jnp.int32)
    nodes = lax.broadcasted_iota(jnp.int32, (mesh_rows, LANES), 0)
    pieces = []
    for row in range(grid_rows // LANES):
        hit = jnp.where(nodes == code[row : row + 1, :], 1.0, 0.0)
        count = count + hit
        pieces.append(hit.astype(BF16))
    total = total + dot(jnp.concatenate(pieces, axis=1), hidden)
    return hidden, total, count


def encode_first_kernel(sign_ref, own_ref, pair_ref, w_in_ref, bias_ref, w_grid_ref, total_ref, count_ref, feat_ref):
    sign = sign_ref[0].astype(F32)
    grid_rows = feat_ref.shape[0]
    bias = bias_ref[...].astype(F32)
    total, count = jnp.zeros(total_ref.shape, F32), jnp.zeros(count_ref.shape, F32)
    hidden, total, count = gather_sums(own_ref, grid_rows, sign, 0, w_in_ref[...], bias, total, count)
    feat_ref[...] = dot(hidden, w_grid_ref[...]).astype(BF16)
    _, total, count = gather_sums(pair_ref, grid_rows, sign, OFFSETS["pair"], w_in_ref[...], bias, total, count)
    total_ref[...] = total
    count_ref[...] = count


def encode_mid_kernel(grid_rows, sign_ref, near_ref, wide_ref, w_in_ref, bias_ref, total_in, count_in, total_ref, count_ref):
    sign = sign_ref[0].astype(F32)
    bias = bias_ref[...].astype(F32)
    total, count = total_in[...], count_in[...]
    for ref, role in ((near_ref, "near"), (wide_ref, "wide")):
        _, total, count = gather_sums(ref, grid_rows, sign, OFFSETS[role], w_in_ref[...], bias, total, count)
    total_ref[...] = total
    count_ref[...] = count


def encode_last_kernel(
    grid_rows, sign_ref, far_ref, w_in_ref, bias_ref, total_in, count_in, w_grid_ref, w_enc_ref, embed_ref, gain_ref,
    state_ref, normed_ref,
):
    sign = sign_ref[0].astype(F32)
    bias = bias_ref[...].astype(F32)
    _, total, count = gather_sums(
        far_ref, grid_rows, sign, OFFSETS["far"], w_in_ref[...], bias, total_in[...], count_in[...]
    )
    counts = jnp.sum(count, axis=1, keepdims=True)
    mean_hidden = (total / jnp.maximum(counts, 1.0)).astype(BF16)
    mean_rows = dot(mean_hidden, w_grid_ref[...]).astype(BF16)
    state = embed_ref[...].astype(F32) + dot(mean_rows, w_enc_ref[...])
    state_ref[...] = state
    normed_ref[...] = rms(state, gain_ref[...].astype(F32)).astype(BF16)


def column(values, index):
    return values[:, index : index + 1]


def attend_blocks(head_dim, pair_index, query_pair, keys, values, allowed, carry):
    rows = query_pair.shape[0]
    low = lax.broadcasted_iota(jnp.int32, (rows, LANES), 1) < head_dim
    lanes = slice(pair_index * LANES, (pair_index + 1) * LANES)
    zero = jnp.zeros_like(query_pair)
    queries = (jnp.where(low, query_pair, zero), jnp.where(low, zero, query_pair))
    scores = [[dot_t(query, key[:, lanes]) * LOG2E for key in keys] for query in queries]
    tops, shifts = [], []
    for half in range(2):
        top = None if carry is None else column(carry[2], half * head_dim)
        for score, allow in zip(scores[half], allowed):
            most = jnp.max(score, axis=1, keepdims=True)
            if allow is not None:
                most = jnp.where(allow, most, -FAR)
            top = most if top is None else jnp.maximum(top, most)
        tops.append(top)
    ones = jnp.ones((keys[0].shape[0], LANES), BF16)
    sums = [None, None]
    for half in range(2):
        for score, allow, value in zip(scores[half], allowed, values):
            shift = tops[half] if allow is None else jnp.where(allow, tops[half], FAR)
            weights = jnp.exp2(score - shift).astype(BF16)
            part = dot(weights, jnp.concatenate([value[:, lanes], ones], axis=1))
            sums[half] = part if sums[half] is None else sums[half] + part
    acc = jnp.where(low, sums[0][:, :LANES], sums[1][:, :LANES])
    norm = jnp.where(low, sums[0][:, LANES:], sums[1][:, LANES:])
    top = jnp.where(low, tops[0], tops[1])
    if carry is not None:
        fade = jnp.exp2(carry[2] - top)
        acc = carry[0] * fade + acc
        norm = carry[1] * fade + norm
    return acc, norm, top


def attend_mid_kernel(
    head_dim, own_ref, pair_ref, near_ref, wide_ref, mask_ref, w_query_ref, w_key_ref, w_value_ref,
    query_ref, acc_ref, norm_ref, top_ref,
):
    mask = mask_ref[...]
    allowed = [None] + [column(mask, index) > 0 for index in (2, 1, 3)]
    query = dot(own_ref[...], w_query_ref[...]).astype(BF16)
    query = query * jnp.asarray(head_dim**-0.5, BF16)
    query_ref[...] = query
    blocks = [own_ref, pair_ref, near_ref, wide_ref]
    keys = [dot(block[...], w_key_ref[...]).astype(BF16) for block in blocks]
    values = [dot(block[...], w_value_ref[...]).astype(BF16) for block in blocks]
    for index in range(query.shape[1] // LANES):
        lanes = slice(index * LANES, (index + 1) * LANES)
        acc, norm, top = attend_blocks(head_dim, index, query[:, lanes], keys, values, allowed, None)
        acc_ref[:, lanes] = acc
        norm_ref[:, lanes] = norm
        top_ref[:, lanes] = top


def attend_last_kernel(
    head_dim, far_ref, mask_ref, w_key_ref, w_value_ref, query_ref, acc_ref, norm_ref, top_ref,
    state_in, w_out_ref, mlp_gain_ref, w_up_ref, w_down_ref, next_gain_ref, state_ref, normed_ref,
):
    allowed = [column(mask_ref[...], 0) > 0]
    keys = [dot(far_ref[...], w_key_ref[...]).astype(BF16)]
    values = [dot(far_ref[...], w_value_ref[...]).astype(BF16)]
    pieces = []
    for index in range(query_ref.shape[1] // LANES):
        lanes = slice(index * LANES, (index + 1) * LANES)
        carry = (acc_ref[:, lanes], norm_ref[:, lanes], top_ref[:, lanes])
        acc, norm, _ = attend_blocks(head_dim, index, query_ref[:, lanes], keys, values, allowed, carry)
        pieces.append((acc / norm).astype(BF16))
    state = state_in[...] + dot(jnp.concatenate(pieces, axis=1), w_out_ref[...])
    normed = rms(state, mlp_gain_ref[...].astype(F32)).astype(BF16)
    up_hidden = silu(dot(normed, w_up_ref[...])).astype(BF16)
    state = state + dot(up_hidden, w_down_ref[...])
    state_ref[...] = state
    normed_ref[...] = rms(state, next_gain_ref[...].astype(F32)).astype(BF16)


def pick_rows(own_ids_ref, sign, role, decoded):
    id_rows = own_ids_ref.shape[0] // 2
    code = jnp.transpose(role_codes(own_ids_ref, sign, role))
    nodes = lax.broadcasted_iota(jnp.int32, (LANES, decoded.shape[0]), 1).astype(F32)
    hits = [jnp.where(nodes == column(code, row), 1.0, 0.0).astype(BF16) for row in range(id_rows)]
    return dot(jnp.concatenate(hits, axis=0), decoded)


def role_codes(ids_ref, sign, role):
    id_rows = ids_ref.shape[0] // 2
    node = ids_ref[pl.ds(0, id_rows), :].astype(F32)
    step = ids_ref[pl.ds(id_rows, id_rows), :].astype(F32) * sign
    return jnp.where(step == float(OFFSETS[role]), node, -1.0)


def decode_mid_kernel(sign_ref, ids_ref, own_ref, pair_ref, near_ref, wide_ref, feat_ref, w_dec_ref, mix_ref):
    sign = sign_ref[0].astype(F32)
    rows = None
    for ref, role in ((own_ref, "own"), (pair_ref, "pair"), (near_ref, "near"), (wide_ref, "wide")):
        part = pick_rows(ids_ref, sign, role, ref[...])
        rows = part if rows is None else rows + part
    mix_ref[...] = feat_ref[...].astype(F32) + dot(rows.astype(BF16), w_dec_ref[...])


def decode_last_kernel(sign_ref, ids_ref, far_ref, mix_ref, w_dec_ref, w_head_ref, w_final_ref, out_ref):
    sign = sign_ref[0].astype(F32)
    rows = pick_rows(ids_ref, sign, "far", far_ref[...]).astype(BF16)
    mix = (mix_ref[...] + dot(rows, w_dec_ref[...])).astype(BF16)
    head_rows = silu(dot(mix, w_head_ref[...])).astype(BF16)
    out_ref[...] = dot(head_rows, w_final_ref[...]).astype(BF16)


def call(kernel, outs, flops, smem=False):
    def run(*operands):
        specs = [pl.BlockSpec(memory_space=pltpu.VMEM) for _ in operands]
        if smem:
            specs[0] = pl.BlockSpec(memory_space=pltpu.SMEM)
        size = sum(o.size * o.dtype.itemsize for o in operands) + sum(
            o.size * o.dtype.itemsize for o in outs
        )
        return pl.pallas_call(
            kernel,
            out_shape=outs,
            in_specs=specs,
            out_specs=[pl.BlockSpec(memory_space=pltpu.VMEM) for _ in outs],
            cost_estimate=pl.CostEstimate(flops=flops, bytes_accessed=size, transcendentals=0),
        )(*operands)

    return run


def shape(rows, columns, dtype):
    return jax.ShapeDtypeStruct((rows, columns), dtype)


def body(
    grid_in, dest_block, dest_node, neighbour_mask, mesh_embed, w_in, in_bias, w_grid, w_enc, attn_gain, w_query,
    w_key, w_value, w_out, mlp_gain, w_up, w_down, dec_gain, w_dec, w_head, w_final,
):
    block_count = lax.axis_size("block")
    me = lax.axis_index("block")
    grid_rows, channels = grid_in.shape
    mesh_rows, width = mesh_embed.shape
    out_width = w_final.shape[1]
    head_dim = width // HEADS
    even = me % 2 == 0
    sign = jnp.where(even, 1, -1).astype(jnp.int32).reshape(1)
    relative = (dest_block[:, 0] - me) % block_count
    relative = jnp.where(relative > block_count // 2, relative - block_count, relative)
    ids = jnp.concatenate(
        [dest_node.reshape(-1, LANES).astype(BF16), relative.reshape(-1, LANES).astype(BF16)], axis=0
    )
    packed = jnp.concatenate([grid_in, ids], axis=0)
    mask = jnp.where(even, neighbour_mask, neighbour_mask[:, ::-1])
    bias = in_bias.reshape(1, -1)

    pair, near, wide, far = spread(packed)
    sums = [shape(mesh_rows, width, F32), shape(mesh_rows, LANES, F32)]
    block_flops = 2 * grid_rows * width * (channels + mesh_rows)
    total, count, feat = call(
        encode_first_kernel, sums + [shape(grid_rows, width, BF16)], 3 * block_flops, True
    )(sign, packed, pair, w_in, bias, w_grid)
    total, count = call(functools.partial(encode_mid_kernel, grid_rows), sums, 2 * block_flops, True)(
        sign, near, wide, w_in, bias, total, count
    )
    states = [shape(mesh_rows, width, F32), shape(mesh_rows, width, BF16)]
    state, normed = call(functools.partial(encode_last_kernel, grid_rows), states, block_flops, True)(
        sign, far, w_in, bias, total, count, w_grid, w_enc, mesh_embed, attn_gain[0:1]
    )
    gains = [attn_gain[layer : layer + 1] for layer in range(1, LAYERS)] + [dec_gain.reshape(1, -1)]
    carries = [shape(mesh_rows, width, BF16)] + [shape(mesh_rows, width, F32)] * 3
    attend_flops = 4 * mesh_rows * width * (width + mesh_rows) * 2
    for layer in range(LAYERS):
        pair, near, wide, far = spread(normed)
        query, acc, norm, top = call(functools.partial(attend_mid_kernel, head_dim), carries, 4 * attend_flops)(
            normed, pair, near, wide, mask, w_query[layer], w_key[layer], w_value[layer]
        )
        state, normed = call(functools.partial(attend_last_kernel, head_dim), states, 2 * attend_flops)(
            far, mask, w_key[layer], w_value[layer], query, acc, norm, top, state,
            w_out[layer], mlp_gain[layer : layer + 1], w_up[layer], w_down[layer], gains[layer],
        )
    pair, near, wide, far = spread(normed)
    (mix,) = call(
        decode_mid_kernel, [shape(grid_rows, width, F32)], 2 * grid_rows * width * (4 * mesh_rows + width), True
    )(sign, ids, normed, pair, near, wide, feat, w_dec)
    (grid_out,) = call(
        decode_last_kernel, [shape(grid_rows, out_width, BF16)], 2 * grid_rows * width * 3 * width, True
    )(sign, ids, far, mix, w_dec, w_head, w_final)
    return grid_out


def solution(mesh):
    split = P(("member", "block"), None)
    placed = (split, split, P(("member", "block")), split, split) + (P(),) * 16
    return jax.shard_map(body, mesh=mesh, in_specs=placed, out_specs=split, check_vma=False)
```

time: 262 us -> 125 us (0.48)
  matrix products: 72.2 us -> 0 us
  Pallas kernels: 0 us -> 62.8 us
  waiting for transfers between devices: 74.9 us -> 17.8 us
  local copies, waits for them, and re-layouts: 63.1 us -> 16.3 us
  starting transfers between devices: 37.2 us -> 24.4 us
  other arithmetic: 11.3 us -> 3.62 us
    dot_general x46 -> x0, matrix products: 72.2 us -> none  [the longest x16 23 us: single(): jnp.dot(softmax_weights, value_head, preferred_element_type=jnp.float32)]
    pallas_call x0 -> x9, Pallas kernels: none -> 62.8 us  [run(): pl.pallas_call(kernel, out_shape=outs, in_specs=specs, out_specs=[pl.Bloc...]
    ppermute x20 -> x16, waiting for transfers between devices: 74.9 us -> 17.8 us  [send(): return lax.ppermute(value, 'block', pairs)]
    gather x3 -> x0, local copies, waits for them, and re-layouts: 20.9 us -> none  [the longest x1 8.2 us: body(): outgoing = padded[source_row].reshape(5, capacity, grid_feat.shape[1])]
    reshape x4 -> x2, local copies, waits for them, and re-layouts: 13.9 us -> 1.14 us  [the longest x1 0.59 us: body(): bias = in_bias.reshape(1, -1)]
    ppermute x20 -> x16, starting transfers between devices: 37.2 us -> 24.4 us  [send(): return lax.ppermute(value, 'block', pairs)]
    scatter x2 -> x0, local copies, waits for them, and re-layouts: 8.81 us -> none  [the longest x1 4.49 us: body(): node_slots = jnp.full((5 * capacity,), -1, jnp.int32).at[placement_index]...]
    broadcast_in_dim x32 -> x0, local copies, waits for them, and re-layouts: 8.05 us -> none  [single(): jnp.where(allowed[:, :, None], scores.reshape(row_count, 5, -1), -jnp.inf)]
  transfers between devices with their start and end apart: 20 -> 16, of which waited for: 7 -> 6; matrix products, arithmetic and copies ran while one was open for 6% -> 9% of each run, Pallas kernels for 0% -> 31%
where the time goes in v1:
time: 125 us
  Pallas kernels  62.8 us (50%)
  starting transfers between devices  24.4 us (20%)
  waiting for transfers between devices  17.8 us (14%)
  local copies, waits for them, and re-layouts  16.3 us (13%)
  other arithmetic  3.62 us (3%)
    pallas_call x9, Pallas kernels, run(): pl.pallas_call(kernel, out_shape=outs, in_specs=specs, out_specs=[pl.Bloc...  62.8 us
    ppermute x16, starting transfers between devices, send(): return lax.ppermute(value, 'block', pairs)  24.4 us
    ppermute x16, waiting for transfers between devices, send(): return lax.ppermute(value, 'block', pairs)  17.8 us
    unnamed x53, local copies, waits for them, and re-layouts  7.29 us
    squeeze x1, local copies, waits for them, and re-layouts, body(): w_query[layer]  3.04 us
  transfers between devices with their start and end apart: 16, of which 6 were waited for; matrix products, arithmetic and copies ran while one was open for 9% of the time, Pallas kernels for 31%

profile of v1, /device:TPU:0, one launch (start us, length us, event | category | flops | bytes accessed | tf_op | source)
XLA Modules:
  0.0 125.1 jit_solution(2978665820170557190)
XLA Ops:
  0.0 0.7 broadcast_subtract_fusion
  0.7 0.7 convert_bitcast_fusion
  1.4 1.0 pad_maximum_fusion.own_ref
  2.4 0.6 collective-permute-start.3
  2.9 5.7 %collective-permute-start.1 = (bf16[1040,128]{1,0:T(8,128)(2,1)S(1)}, bf16[1040,128]{1,0:T(8,128)(2,1)S(1)}, u32[]{:S(2)}, u32[]{:S(2)}) collective-permute-start(bf16[1040,128]{1,0:T(8,128)(2,1)S(1)} %pad_maximum_fusion.own_ref), channel_id=1, source_target_pairs={{0,15},{1,2},{2,1},{3,4},{4,3},{5,6},{6,5},{7,8},{8,7},{9,10},{10,... | collective-permute-start | bytes 798728 | tf_op jit(solution)/shard_map/ppermute | solution.py:28
  8.6 0.0 collective-permute-start
  8.6 0.8 copy.23
  9.4 0.2 rev.3
  9.6 0.0 copy-start.2
  9.6 0.0 copy-start.3
  9.6 3.0 %slice_bitcast_fusion.3 = (bf16[512,512]{1,0:T(8,128)(2,1)}, bf16[512,512]{1,0:T(8,128)(2,1)}, bf16[512,512]{1,0:T(8,128)(2,1)}, bf16[512,512]{1,0:T(8,128)(2,1)}) fusion(bf16[2,512,512]{2,1,0:T(8,128)(2,1)} %param.31, bf16[2,512,512]{2,1,0:T(8,128)(2,1)} %param.33), kind=kLoop, calls=%fused_computation.3 | loop fusion | bytes 4194304 | tf_op jit(solution)/shard_map/squeeze | solution.py:291
  12.7 0.0 copy-start.6
  12.7 0.0 copy-start.7
  12.7 0.0 copy-start.8
  12.7 1.3 %slice_bitcast_fusion = (bf16[512,512]{1,0:T(8,128)(2,1)}, bf16[512,512]{1,0:T(8,128)(2,1)}, bf16[512,512]{1,0:T(8,128)(2,1)}, bf16[512,512]{1,0:T(8,128)(2,1)}) fusion(bf16[2,512,512]{2,1,0:T(8,128)(2,1)S(1)} %copy-done.2, bf16[2,512,512]{2,1,0:T(8,128)(2,1)S(1)} %copy-done.3), kind=kLoop, calls=%fused_computation | loop fusion | bytes 4194304 | tf_op jit(solution)/shard_map/squeeze | solution.py:295
  14.1 0.7 broadcast_select_fusion.mask_ref
  14.7 0.6 fusion.3
  15.3 0.0 collective-permute-done.1.near_ref
  15.3 0.6 collective-permute-start.2
  15.9 0.6 fusion.2
  16.5 0.6 reshape.16.bias_ref
  17.1 0.7 copy-done.11
  17.8 4.5 %shard_map.199 = (f32[256,512]{1,0:T(8,128)}, f32[256,128]{1,0:T(8,128)}, bf16[1024,512]{1,0:T(8,128)(2,1)}) custom-call(s32[1]{0:T(128)} %bitcast.sign_ref, bf16[1040,128]{1,0:T(8,128)(2,1)} %copy-done.4, bf16[1040,128]{1,0:T(8,128)(2,1)} %copy-done.11, bf16[128,512]{1,0:T(8,128)(2,1)} %w_in_ref.5, bf16[1,512]{1,0:T(2,128)(2,1)} %reshape.16.bias_ref, ...), custom_call_target="tpu_custom_call" | custom-call | flops 1207959552 | bytes 2892804 | tf_op jit(solution)/shard_map/pallas_call | solution.py:236
  22.4 0.0 collective-permute-done.2.wide_ref
  22.4 0.7 copy-done.12
  23.1 3.9 %shard_map.200 = (f32[256,512]{1,0:T(8,128)}, f32[256,128]{1,0:T(8,128)}) custom-call(s32[1]{0:T(128)} %bitcast.sign_ref, bf16[1040,128]{1,0:T(8,128)(2,1)} %copy-done.10, bf16[1040,128]{1,0:T(8,128)(2,1)} %copy-done.12, bf16[128,512]{1,0:T(8,128)(2,1)} %w_in_ref.5, bf16[1,512]{1,0:T(2,128)(2,1)} %reshape.16.bias_ref, ...), custom_call_target="tpu_custom_call" | custom-call | flops 805306368 | bytes 1975300 | tf_op jit(solution)/shard_map/pallas_call | solution.py:236
  27.0 0.7 copy-done.5
  27.7 3.9 %shard_map.201 = (f32[256,512]{1,0:T(8,128)}, bf16[256,512]{1,0:T(8,128)(2,1)}) custom-call(s32[1]{0:T(128)} %bitcast.sign_ref, bf16[1040,128]{1,0:T(8,128)(2,1)} %copy-done.5, bf16[128,512]{1,0:T(8,128)(2,1)} %w_in_ref.5, bf16[1,512]{1,0:T(2,128)(2,1)} %reshape.16.bias_ref, f32[256,512]{1,0:T(8,128)} %get-tuple-element.25.total_in, ...), custom_call_target="tpu_custom_call" | custom-call | flops 402653184 | bytes 3151876 | tf_op jit(solution)/shard_map/pallas_call | solution.py:236
  31.7 6.0 %collective-permute-start.6 = (bf16[256,512]{1,0:T(8,128)(2,1)}, bf16[256,512]{1,0:T(8,128)(2,1)S(1)}, u32[]{:S(2)}, u32[]{:S(2)}) collective-permute-start(bf16[256,512]{1,0:T(8,128)(2,1)} %get-tuple-element.27.own_ref), channel_id=1, source_target_pairs={{0,15},{1,2},{2,1},{3,4},{4,3},{5,6},{6,5},{7,8},{8,7},{9,10},{10,... | collective-permute-start | bytes 786440 | tf_op jit(solution)/shard_map/ppermute | solution.py:28
  37.7 1.1 slice_bitcast_fusion.5
  38.7 3.3 %collective-permute-done.6.near_ref = bf16[256,512]{1,0:T(8,128)(2,1)S(1)} collective-permute-done((bf16[256,512]{1,0:T(8,128)(2,1)}, bf16[256,512]{1,0:T(8,128)(2,1)S(1)}, u32[]{:S(2)}, u32[]{:S(2)}) %collective-permute-start.6) | collective-permute-done | bytes 262176 | tf_op jit(solution)/shard_map/ppermute | solution.py:28
  42.0 0.0 collective-permute-start.7
  42.0 1.1 slice_bitcast_fusion.2
  43.1 0.9 collective-permute-start.4
  44.0 0.7 copy-done.18
  44.7 0.1 copy-done.22
  44.8 12.7 %shard_map.202 = (bf16[256,512]{1,0:T(8,128)(2,1)}, f32[256,512]{1,0:T(8,128)}, f32[256,512]{1,0:T(8,128)}, f32[256,512]{1,0:T(8,128)}) custom-call(bf16[256,512]{1,0:T(8,128)(2,1)} %get-tuple-element.27.own_ref, bf16[256,512]{1,0:T(8,128)(2,1)} %copy-done.18, bf16[256,512]{1,0:T(8,128)(2,1)} %copy-done.15, bf16[256,512]{1,0:T(8,128)(2,1)} %copy-done.22, ...), custom_call_target="tpu_custom_call" | custom-call | flops 3221225472 | bytes 4460544 | tf_op jit(solution)/shard_map/pallas_call | solution.py:236
  57.5 0.7 copy-done.16
  58.2 7.7 %shard_map.203 = (f32[256,512]{1,0:T(8,128)}, bf16[256,512]{1,0:T(8,128)(2,1)}) custom-call(bf16[256,512]{1,0:T(8,128)(2,1)} %copy-done.16, s32[256,4]{1,0:T(8,128)} %broadcast_select_fusion.mask_ref, bf16[512,512]{1,0:T(8,128)(2,1)} %get-tuple-element.52.w_key_ref, bf16[512,512]{1,0:T(8,128)(2,1)} %get-tuple-element.57.w_value_ref, ...), custom_call_target="tpu_custom_call" | custom-call | flops 1610612736 | bytes 6035456 | tf_op jit(solution)/shard_map/pallas_call | solution.py:236
  65.9 4.5 %collective-permute-start.10 = (bf16[256,512]{1,0:T(8,128)(2,1)}, bf16[256,512]{1,0:T(8,128)(2,1)S(1)}, u32[]{:S(2)}, u32[]{:S(2)}) collective-permute-start(bf16[256,512]{1,0:T(8,128)(2,1)} %get-tuple-element.33.own_ref), channel_id=1, source_target_pairs={{0,15},{1,2},{2,1},{3,4},{4,3},{5,6},{6,5},{7,8},{8,7},{9,10},{10,... | collective-permute-start | bytes 786440 | tf_op jit(solution)/shard_map/ppermute | solution.py:28
  70.4 0.0 collective-permute-start.9
  70.4 4.4 %collective-permute-done.10.near_ref = bf16[256,512]{1,0:T(8,128)(2,1)S(1)} collective-permute-done((bf16[256,512]{1,0:T(8,128)(2,1)}, bf16[256,512]{1,0:T(8,128)(2,1)S(1)}, u32[]{:S(2)}, u32[]{:S(2)}) %collective-permute-start.10) | collective-permute-done | bytes 262176 | tf_op jit(solution)/shard_map/ppermute | solution.py:28
  74.8 2.5 %collective-permute-start.11 = (bf16[256,512]{1,0:T(8,128)(2,1)S(1)}, bf16[256,512]{1,0:T(8,128)(2,1)S(1)}, u32[]{:S(2)}, u32[]{:S(2)}) collective-permute-start(bf16[256,512]{1,0:T(8,128)(2,1)S(1)} %collective-permute-done.10.near_ref), channel_id=1, source_target_pairs={{0,1},{1,0},{2,3},{3,2},{4,5},{5,4},{6,7},{7,6},{8,9},{9,8},{10,11... | collective-permute-start | bytes 786440 | tf_op jit(solution)/shard_map/ppermute | solution.py:28
  77.3 0.5 reshape.17.next_gain_ref
  77.9 0.0 collective-permute-start.8
  77.9 0.6 collective-permute-done.11.wide_ref
  78.5 0.1 copy-done.19
  78.6 0.6 copy-done.23
  79.2 12.6 %shard_map.204 = (bf16[256,512]{1,0:T(8,128)(2,1)}, f32[256,512]{1,0:T(8,128)}, f32[256,512]{1,0:T(8,128)}, f32[256,512]{1,0:T(8,128)}) custom-call(bf16[256,512]{1,0:T(8,128)(2,1)} %get-tuple-element.33.own_ref, bf16[256,512]{1,0:T(8,128)(2,1)} %copy-done.19, bf16[256,512]{1,0:T(8,128)(2,1)} %copy-done.17, bf16[256,512]{1,0:T(8,128)(2,1)} %copy-done.23, ...), custom_call_target="tpu_custom_call" | custom-call | flops 3221225472 | bytes 4460544 | tf_op jit(solution)/shard_map/pallas_call | solution.py:236
  91.8 0.7 copy-done.14
  92.5 7.7 %shard_map.205 = (f32[256,512]{1,0:T(8,128)}, bf16[256,512]{1,0:T(8,128)(2,1)}) custom-call(bf16[256,512]{1,0:T(8,128)(2,1)} %copy-done.14, s32[256,4]{1,0:T(8,128)} %broadcast_select_fusion.mask_ref, bf16[512,512]{1,0:T(8,128)(2,1)} %get-tuple-element.51.w_key_ref, bf16[512,512]{1,0:T(8,128)(2,1)} %get-tuple-element.58.w_value_ref, ...), custom_call_target="tpu_custom_call" | custom-call | flops 1610612736 | bytes 6035456 | tf_op jit(solution)/shard_map/pallas_call | solution.py:236
  100.1 2.2 %collective-permute-start.14 = (bf16[256,512]{1,0:T(8,128)(2,1)}, bf16[256,512]{1,0:T(8,128)(2,1)S(1)}, u32[]{:S(2)}, u32[]{:S(2)}) collective-permute-start(bf16[256,512]{1,0:T(8,128)(2,1)} %get-tuple-element.39.own_ref), channel_id=1, source_target_pairs={{0,15},{1,2},{2,1},{3,4},{4,3},{5,6},{6,5},{7,8},{8,7},{9,10},{10,... | collective-permute-start | bytes 786440 | tf_op jit(solution)/shard_map/ppermute | solution.py:28
  102.3 0.0 collective-permute-start.13
  102.3 6.6 %collective-permute-done.14.near_ref = bf16[256,512]{1,0:T(8,128)(2,1)S(1)} collective-permute-done((bf16[256,512]{1,0:T(8,128)(2,1)}, bf16[256,512]{1,0:T(8,128)(2,1)S(1)}, u32[]{:S(2)}, u32[]{:S(2)}) %collective-permute-start.14) | collective-permute-done | bytes 262176 | tf_op jit(solution)/shard_map/ppermute | solution.py:28
  109.0 1.5 %collective-permute-start.15 = (bf16[256,512]{1,0:T(8,128)(2,1)S(1)}, bf16[256,512]{1,0:T(8,128)(2,1)S(1)}, u32[]{:S(2)}, u32[]{:S(2)}) collective-permute-start(bf16[256,512]{1,0:T(8,128)(2,1)S(1)} %collective-permute-done.14.near_ref), channel_id=1, source_target_pairs={{0,1},{1,0},{2,3},{3,2},{4,5},{5,4},{6,7},{7,6},{8,9},{9,8},{10,11... | collective-permute-start | bytes 786440 | tf_op jit(solution)/shard_map/ppermute | solution.py:28
  110.4 0.0 collective-permute-start.12
  110.4 0.6 pad_maximum_fusion.1.ids_ref
  111.0 0.6 collective-permute-done.15.wide_ref
  111.6 0.1 copy-done.21
  111.7 0.6 copy-done.25
  112.3 5.1 %shard_map.206.mix_ref = f32[1024,512]{1,0:T(8,128)} custom-call(s32[1]{0:T(128)} %bitcast.sign_ref, bf16[16,128]{1,0:T(8,128)(2,1)} %pad_maximum_fusion.1.ids_ref, bf16[256,512]{1,0:T(8,128)(2,1)} %get-tuple-element.39.own_ref, bf16[256,512]{1,0:T(8,128)(2,1)} %copy-done.21, bf16[256,512]{1,0:T(8,128)(2,1)} %copy-done.20, bf16[256,512]{1,0:T(8,128)(2,1)} %copy-done.25, ...), custom_call_target="tpu_custom_call" | custom-call | flops 1610612736 | bytes 4722692 | tf_op jit(solution)/shard_map/pallas_call | solution.py:236
  117.4 2.3 %collective-permute-done.12.far_ref = bf16[256,512]{1,0:T(8,128)(2,1)S(1)} collective-permute-done((bf16[256,512]{1,0:T(8,128)(2,1)}, bf16[256,512]{1,0:T(8,128)(2,1)S(1)}, u32[]{:S(2)}, u32[]{:S(2)}) %collective-permute-start.12) | collective-permute-done | bytes 262176 | tf_op jit(solution)/shard_map/ppermute | solution.py:28
  119.7 0.7 copy-done.24
  120.4 4.7 %shard_map.207 = bf16[1024,128]{1,0:T(8,128)(2,1)} custom-call(s32[1]{0:T(128)} %bitcast.sign_ref, bf16[16,128]{1,0:T(8,128)(2,1)} %pad_maximum_fusion.1.ids_ref, bf16[256,512]{1,0:T(8,128)(2,1)} %copy-done.24, f32[1024,512]{1,0:T(8,128)} %shard_map.206.mix_ref, bf16[512,512]{1,0:T(8,128)(2,1)} %w_dec_ref.3, bf16[512,512]{1,0:T(8,128)(2,1)} %w_head_ref.1, ...), custom_call_target="tpu_custom_call" | custom-call | flops 1610612736 | bytes 3805188 | tf_op jit(solution)/shard_map/pallas_call | solution.py:236
  (45 shorter events, 0.1 us)
Async XLA Ops:
  2.4 10.3 %copy-start.4 = (bf16[1040,128]{1,0:T(8,128)(2,1)}, bf16[1040,128]{1,0:T(8,128)(2,1)S(1)}, u32[]{:S(2)}) copy-start(bf16[1040,128]{1,0:T(8,128)(2,1)S(1)} %pad_maximum_fusion.own_ref) | copy-start | bytes 798724
  2.4 14.8 %collective-permute-start.3 = (bf16[1040,128]{1,0:T(8,128)(2,1)S(1)}, bf16[1040,128]{1,0:T(8,128)(2,1)S(1)}, u32[]{:S(2)}, u32[]{:S(2)}) collective-permute-start(bf16[1040,128]{1,0:T(8,128)(2,1)S(1)} %pad_maximum_fusion.own_ref), channel_id=1, source_target_pairs={{0,1},{1,0},{2,3},{3,2},{4,5},{5,4},{6,7},{7,6},{8,9},{9,8},{10,11... | collective-permute-start | bytes 798728 | tf_op jit(solution)/shard_map/ppermute | solution.py:28
  2.9 12.4 %collective-permute-start.1 = (bf16[1040,128]{1,0:T(8,128)(2,1)S(1)}, bf16[1040,128]{1,0:T(8,128)(2,1)S(1)}, u32[]{:S(2)}, u32[]{:S(2)}) collective-permute-start(bf16[1040,128]{1,0:T(8,128)(2,1)S(1)} %pad_maximum_fusion.own_ref), channel_id=1, source_target_pairs={{0,15},{1,2},{2,1},{3,4},{4,3},{5,6},{6,5},{7,8},{8,7},{9,10},{10,... | collective-permute-start | bytes 798728 | tf_op jit(solution)/shard_map/ppermute | solution.py:28
  8.6 18.4 %collective-permute-start = (bf16[1040,128]{1,0:T(8,128)(2,1)S(1)}, bf16[1040,128]{1,0:T(8,128)(2,1)S(1)}, u32[]{:S(2)}, u32[]{:S(2)}) collective-permute-start(bf16[1040,128]{1,0:T(8,128)(2,1)S(1)} %pad_maximum_fusion.own_ref), channel_id=1, source_target_pairs={{0,2},{1,15},{2,4},{3,1},{4,6},{5,3},{6,8},{7,5},{8,10},{9,7},{10,... | collective-permute-start | bytes 798728 | tf_op jit(solution)/shard_map/ppermute | solution.py:28
  9.6 3.1 %copy-start.2 = (bf16[2,512,512]{2,1,0:T(8,128)(2,1)S(1)}, bf16[2,512,512]{2,1,0:T(8,128)(2,1)}, u32[]{:S(2)}) copy-start(bf16[2,512,512]{2,1,0:T(8,128)(2,1)} %param.37) | copy-start | bytes 3145732
  9.6 3.1 %copy-start.3 = (bf16[2,512,512]{2,1,0:T(8,128)(2,1)S(1)}, bf16[2,512,512]{2,1,0:T(8,128)(2,1)}, u32[]{:S(2)}) copy-start(bf16[2,512,512]{2,1,0:T(8,128)(2,1)} %param.36) | copy-start | bytes 3145732
  12.7 2.0 %copy-start.6 = (bf16[2,512]{1,0:T(2,128)(2,1)S(1)}, bf16[2,512]{1,0:T(2,128)(2,1)}, u32[]{:S(2)}) copy-start(bf16[2,512]{1,0:T(2,128)(2,1)} %param.30) | copy-start | bytes 6148
  12.7 3.3 %copy-start.7 = (bf16[2,512]{1,0:T(2,128)(2,1)S(1)}, bf16[2,512]{1,0:T(2,128)(2,1)}, u32[]{:S(2)}) copy-start(bf16[2,512]{1,0:T(2,128)(2,1)} %param.35) | copy-start | bytes 6148
  12.7 3.8 %copy-start.8 = (bf16[512]{0:T(512)(128)(2,1)S(1)}, bf16[512]{0:T(512)(128)(2,1)}, u32[]{:S(2)}) copy-start(bf16[512]{0:T(512)(128)(2,1)} %param.27) | copy-start | bytes 3076
  15.3 7.0 %copy-start.10 = (bf16[1040,128]{1,0:T(8,128)(2,1)}, bf16[1040,128]{1,0:T(8,128)(2,1)S(1)}, u32[]{:S(2)}) copy-start(bf16[1040,128]{1,0:T(8,128)(2,1)S(1)} %collective-permute-done.1.near_ref) | copy-start | bytes 798724
  15.3 7.0 %collective-permute-start.2 = (bf16[1040,128]{1,0:T(8,128)(2,1)S(1)}, bf16[1040,128]{1,0:T(8,128)(2,1)S(1)}, u32[]{:S(2)}, u32[]{:S(2)}) collective-permute-start(bf16[1040,128]{1,0:T(8,128)(2,1)S(1)} %collective-permute-done.1.near_ref), channel_id=1, source_target_pairs={{0,1},{1,0},{2,3},{3,2},{4,5},{5,4},{6,7},{7,6},{8,9},{9,8},{10,11... | collective-permute-start | bytes 798728 | tf_op jit(solution)/shard_map/ppermute | solution.py:28
  17.1 0.7 copy-start.11
  22.4 0.7 copy-start.12
  23.1 14.6 %copy-start = (bf16[2,512,512]{2,1,0:T(8,128)(2,1)S(1)}, bf16[2,512,512]{2,1,0:T(8,128)(2,1)}, u32[]{:S(2)}) copy-start(bf16[2,512,512]{2,1,0:T(8,128)(2,1)} %param.32) | copy-start | bytes 3145732
  27.0 0.7 copy-start.5
  27.7 14.3 %copy-start.1 = (bf16[2,512,512]{2,1,0:T(8,128)(2,1)S(1)}, bf16[2,512,512]{2,1,0:T(8,128)(2,1)}, u32[]{:S(2)}) copy-start(bf16[2,512,512]{2,1,0:T(8,128)(2,1)} %param.34) | copy-start | bytes 3145732
  31.7 7.1 %copy-start.13 = (bf16[256,512]{1,0:T(8,128)(2,1)S(1)}, bf16[256,512]{1,0:T(8,128)(2,1)}, u32[]{:S(2)}) copy-start(bf16[256,512]{1,0:T(8,128)(2,1)} %get-tuple-element.27.own_ref) | copy-start | bytes 786436
  31.7 10.3 %collective-permute-start.6 = (bf16[256,512]{1,0:T(8,128)(2,1)}, bf16[256,512]{1,0:T(8,128)(2,1)S(1)}, u32[]{:S(2)}, u32[]{:S(2)}) collective-permute-start(bf16[256,512]{1,0:T(8,128)(2,1)} %get-tuple-element.27.own_ref), channel_id=1, source_target_pairs={{0,15},{1,2},{2,1},{3,4},{4,3},{5,6},{6,5},{7,8},{8,7},{9,10},{10,... | collective-permute-start | bytes 786440 | tf_op jit(solution)/shard_map/ppermute | solution.py:28
  38.7 5.3 %collective-permute-start.5 = (bf16[256,512]{1,0:T(8,128)(2,1)S(1)}, bf16[256,512]{1,0:T(8,128)(2,1)S(1)}, u32[]{:S(2)}, u32[]{:S(2)}) collective-permute-start(bf16[256,512]{1,0:T(8,128)(2,1)S(1)} %copy-done.13), channel_id=1, source_target_pairs={{0,1},{1,0},{2,3},{3,2},{4,5},{5,4},{6,7},{7,6},{8,9},{9,8},{10,11... | collective-permute-start | bytes 786440 | tf_op jit(solution)/shard_map/ppermute | solution.py:28
  42.0 2.0 %copy-start.15 = (bf16[256,512]{1,0:T(8,128)(2,1)}, bf16[256,512]{1,0:T(8,128)(2,1)S(1)}, u32[]{:S(2)}) copy-start(bf16[256,512]{1,0:T(8,128)(2,1)S(1)} %collective-permute-done.6.near_ref) | copy-start | bytes 786436
  42.0 2.0 %collective-permute-start.7 = (bf16[256,512]{1,0:T(8,128)(2,1)S(1)}, bf16[256,512]{1,0:T(8,128)(2,1)S(1)}, u32[]{:S(2)}, u32[]{:S(2)}) collective-permute-start(bf16[256,512]{1,0:T(8,128)(2,1)S(1)} %collective-permute-done.6.near_ref), channel_id=1, source_target_pairs={{0,1},{1,0},{2,3},{3,2},{4,5},{5,4},{6,7},{7,6},{8,9},{9,8},{10,11... | collective-permute-start | bytes 786440 | tf_op jit(solution)/shard_map/ppermute | solution.py:28
  43.1 14.4 %collective-permute-start.4 = (bf16[256,512]{1,0:T(8,128)(2,1)S(1)}, bf16[256,512]{1,0:T(8,128)(2,1)S(1)}, u32[]{:S(2)}, u32[]{:S(2)}) collective-permute-start(bf16[256,512]{1,0:T(8,128)(2,1)S(1)} %copy-done.13), channel_id=1, source_target_pairs={{0,2},{1,15},{2,4},{3,1},{4,6},{5,3},{6,8},{7,5},{8,10},{9,7},{10,... | collective-permute-start | bytes 786440 | tf_op jit(solution)/shard_map/ppermute | solution.py:28
  44.0 0.7 copy-start.18
  44.0 0.8 copy-start.22
  57.5 0.7 copy-start.16
  58.2 19.1 %copy-start.9 = (bf16[512]{0:T(512)(128)(2,1)S(1)}, bf16[512]{0:T(512)(128)(2,1)}, u32[]{:S(2)}) copy-start(bf16[512]{0:T(512)(128)(2,1)} %param.38) | copy-start | bytes 3076
  65.9 8.9 %collective-permute-start.10 = (bf16[256,512]{1,0:T(8,128)(2,1)}, bf16[256,512]{1,0:T(8,128)(2,1)S(1)}, u32[]{:S(2)}, u32[]{:S(2)}) collective-permute-start(bf16[256,512]{1,0:T(8,128)(2,1)} %get-tuple-element.33.own_ref), channel_id=1, source_target_pairs={{0,15},{1,2},{2,1},{3,4},{4,3},{5,6},{6,5},{7,8},{8,7},{9,10},{10,... | collective-permute-start | bytes 786440 | tf_op jit(solution)/shard_map/ppermute | solution.py:28
  70.4 7.5 %collective-permute-start.9 = (bf16[256,512]{1,0:T(8,128)(2,1)}, bf16[256,512]{1,0:T(8,128)(2,1)S(1)}, u32[]{:S(2)}, u32[]{:S(2)}) collective-permute-start(bf16[256,512]{1,0:T(8,128)(2,1)} %get-tuple-element.33.own_ref), channel_id=1, source_target_pairs={{0,1},{1,0},{2,3},{3,2},{4,5},{5,4},{6,7},{7,6},{8,9},{9,8},{10,11... | collective-permute-start | bytes 786440 | tf_op jit(solution)/shard_map/ppermute | solution.py:28
  74.8 3.7 %copy-start.17 = (bf16[256,512]{1,0:T(8,128)(2,1)}, bf16[256,512]{1,0:T(8,128)(2,1)S(1)}, u32[]{:S(2)}) copy-start(bf16[256,512]{1,0:T(8,128)(2,1)S(1)} %collective-permute-done.10.near_ref) | copy-start | bytes 786436
  74.8 3.7 %collective-permute-start.11 = (bf16[256,512]{1,0:T(8,128)(2,1)S(1)}, bf16[256,512]{1,0:T(8,128)(2,1)S(1)}, u32[]{:S(2)}, u32[]{:S(2)}) collective-permute-start(bf16[256,512]{1,0:T(8,128)(2,1)S(1)} %collective-permute-done.10.near_ref), channel_id=1, source_target_pairs={{0,1},{1,0},{2,3},{3,2},{4,5},{5,4},{6,7},{7,6},{8,9},{9,8},{10,11... | collective-permute-start | bytes 786440 | tf_op jit(solution)/shard_map/ppermute | solution.py:28
  77.9 13.9 %collective-permute-start.8 = (bf16[256,512]{1,0:T(8,128)(2,1)}, bf16[256,512]{1,0:T(8,128)(2,1)S(1)}, u32[]{:S(2)}, u32[]{:S(2)}) collective-permute-start(bf16[256,512]{1,0:T(8,128)(2,1)} %get-tuple-element.33.own_ref), channel_id=1, source_target_pairs={{0,2},{1,15},{2,4},{3,1},{4,6},{5,3},{6,8},{7,5},{8,10},{9,7},{10,... | collective-permute-start | bytes 786440 | tf_op jit(solution)/shard_map/ppermute | solution.py:28
  77.9 0.7 copy-start.19
  78.5 0.7 copy-start.23
  91.7 0.7 copy-start.14
  100.1 8.8 %collective-permute-start.14 = (bf16[256,512]{1,0:T(8,128)(2,1)}, bf16[256,512]{1,0:T(8,128)(2,1)S(1)}, u32[]{:S(2)}, u32[]{:S(2)}) collective-permute-start(bf16[256,512]{1,0:T(8,128)(2,1)} %get-tuple-element.39.own_ref), channel_id=1, source_target_pairs={{0,15},{1,2},{2,1},{3,4},{4,3},{5,6},{6,5},{7,8},{8,7},{9,10},{10,... | collective-permute-start | bytes 786440 | tf_op jit(solution)/shard_map/ppermute | solution.py:28
  102.3 8.7 %collective-permute-start.13 = (bf16[256,512]{1,0:T(8,128)(2,1)}, bf16[256,512]{1,0:T(8,128)(2,1)S(1)}, u32[]{:S(2)}, u32[]{:S(2)}) collective-permute-start(bf16[256,512]{1,0:T(8,128)(2,1)} %get-tuple-element.39.own_ref), channel_id=1, source_target_pairs={{0,1},{1,0},{2,3},{3,2},{4,5},{5,4},{6,7},{7,6},{8,9},{9,8},{10,11... | collective-permute-start | bytes 786440 | tf_op jit(solution)/shard_map/ppermute | solution.py:28
  108.9 2.6 %copy-start.20 = (bf16[256,512]{1,0:T(8,128)(2,1)}, bf16[256,512]{1,0:T(8,128)(2,1)S(1)}, u32[]{:S(2)}) copy-start(bf16[256,512]{1,0:T(8,128)(2,1)S(1)} %collective-permute-done.14.near_ref) | copy-start | bytes 786436
  109.0 2.6 %collective-permute-start.15 = (bf16[256,512]{1,0:T(8,128)(2,1)S(1)}, bf16[256,512]{1,0:T(8,128)(2,1)S(1)}, u32[]{:S(2)}, u32[]{:S(2)}) collective-permute-start(bf16[256,512]{1,0:T(8,128)(2,1)S(1)} %collective-permute-done.14.near_ref), channel_id=1, source_target_pairs={{0,1},{1,0},{2,3},{3,2},{4,5},{5,4},{6,7},{7,6},{8,9},{9,8},{10,11... | collective-permute-start | bytes 786440 | tf_op jit(solution)/shard_map/ppermute | solution.py:28
  110.4 9.3 %collective-permute-start.12 = (bf16[256,512]{1,0:T(8,128)(2,1)}, bf16[256,512]{1,0:T(8,128)(2,1)S(1)}, u32[]{:S(2)}, u32[]{:S(2)}) collective-permute-start(bf16[256,512]{1,0:T(8,128)(2,1)} %get-tuple-element.39.own_ref), channel_id=1, source_target_pairs={{0,2},{1,15},{2,4},{3,1},{4,6},{5,3},{6,8},{7,5},{8,10},{9,7},{10,... | collective-permute-start | bytes 786440 | tf_op jit(solution)/shard_map/ppermute | solution.py:28
  111.0 0.7 copy-start.21
  111.6 0.7 copy-start.25
  119.7 0.7 copy-start.24

commit v2 on v1

v2 whole, which is shorter than its diff:
```python
import functools

import jax
import jax.numpy as jnp
import numpy as np
from jax import lax
from jax.experimental import pallas as pl
from jax.experimental.pallas import tpu as pltpu
from jax.sharding import PartitionSpec as P

HEADS = 8
LAYERS = 2
LANES = 128
BF16 = jnp.bfloat16
F32 = jnp.float32
LOG2E = 1.4426950408889634
FAR = 1e30
KERNEL_VMEM = 24 * 1024 * 1024


OFFSETS = {"own": 0, "pair": 1, "near": -1, "wide": 2, "far": -2}


def send(value, step_even, step_odd):
    count = lax.axis_size("block")
    pairs = [
        (source, (source + (step_even if source % 2 == 0 else step_odd)) % count)
        for source in range(count)
    ]
    return lax.ppermute(value, "block", pairs)


def spread(value):
    near = send(value, -1, 1)
    far = send(value, 2, -2)
    pair = send(value, 1, -1)
    wide = send(near, 1, -1)
    return pair, near, wide, far


def dot(left, right):
    return lax.dot_general(left, right, (((1,), (0,)), ((), ())), preferred_element_type=F32)


def dot_t(left, right):
    return lax.dot_general(left, right, (((1,), (1,)), ((), ())), preferred_element_type=F32)


def silu(values):
    half = 0.5 * values
    return half * (jnp.tanh(half) + 1.0)


def rms(values, gain):
    mean = jnp.mean(values * values, axis=-1, keepdims=True)
    return values * lax.rsqrt(mean + 1e-06) * gain


def parity(me_ref):
    return lax.rem(me_ref[0], 2)


def offset_of(role, odd):
    return OFFSETS[role] * (1 - 2 * odd)


def pack_kernel(block_count, me_ref, grid_ref, block_ref, node_ref, packed_ref, ids_ref):
    grid_rows = grid_ref.shape[0]
    relative = block_ref[...] - me_ref[0]
    relative = jnp.where(relative > 2, relative - block_count, relative)
    relative = jnp.where(relative < -2, relative + block_count, relative)
    ids = jnp.concatenate([node_ref[...].astype(F32), relative.astype(F32)], axis=0).astype(BF16)
    ids_ref[...] = ids
    packed_ref[pl.ds(0, grid_rows), :] = grid_ref[...]
    packed_ref[pl.ds(grid_rows, ids.shape[0]), :] = ids


def node_sums(packed_ref, grid_rows, offset, w_in, bias, total, count):
    mesh_rows = total.shape[0]
    id_rows = grid_rows // LANES
    hidden = silu(dot(packed_ref[pl.ds(0, grid_rows), :], w_in) + bias).astype(BF16)
    ids = packed_ref[pl.ds(grid_rows, 2 * id_rows), :].astype(F32)
    code = jnp.where(ids[id_rows:] == -offset.astype(F32), ids[:id_rows], -1.0).astype(jnp.int32)
    nodes = lax.broadcasted_iota(jnp.int32, (mesh_rows, LANES), 0)
    pieces = []
    for row in range(id_rows):
        hit = jnp.where(nodes == code[row : row + 1, :], 1.0, 0.0)
        count = count + hit
        pieces.append(hit.astype(BF16))
    total = total + dot(jnp.concatenate(pieces, axis=1), hidden)
    return hidden, total, count


def encode_kernel(roles, grid_rows, me_ref, *refs):
    odd = parity(me_ref)
    blocks, refs = refs[: len(roles)], refs[len(roles) :]
    w_in_ref, bias_ref, refs = refs[0], refs[1], refs[2:]
    bias = bias_ref[...].astype(F32)
    first, last = roles[0] == "own", roles[-1] == "far"
    if first:
        w_grid_ref, mask_ref, total_ref, count_ref, feat_ref, gate_ref = refs
        total, count = jnp.zeros(total_ref.shape, F32), jnp.zeros(count_ref.shape, F32)
        closed = jnp.where(mask_ref[...] > 0, 0.0, -FAR)
        closed = jnp.concatenate([closed, jnp.zeros((LANES - closed.shape[0], closed.shape[1]), F32)], axis=0)
        gate_ref[...] = jnp.transpose(closed).astype(BF16)
    elif last:
        total_in, count_in, w_grid_ref, w_enc_ref, embed_ref, gain_ref, state_ref, normed_ref = refs
        total, count = total_in[...], count_in[...]
    else:
        total_in, count_in, total_ref, count_ref = refs
        total, count = total_in[...], count_in[...]
    for role, ref in zip(roles, blocks):
        hidden, total, count = node_sums(
            ref, grid_rows, offset_of(role, odd), w_in_ref[...], bias, total, count
        )
        if role == "own":
            feat_ref[...] = dot(hidden, w_grid_ref[...]).astype(BF16)
    if not last:
        total_ref[...] = total
        count_ref[...] = count
        return
    counts = jnp.sum(count, axis=1, keepdims=True)
    mean_hidden = (total / jnp.maximum(counts, 1.0)).astype(BF16)
    mean_rows = dot(mean_hidden, w_grid_ref[...]).astype(BF16)
    state = embed_ref[...].astype(F32) + dot(mean_rows, w_enc_ref[...])
    state_ref[...] = state
    normed_ref[...] = rms(state, gain_ref[0:1, :].astype(F32)).astype(BF16)


def key_gate(role, odd, rows):
    lane = lax.broadcasted_iota(jnp.int32, (rows, LANES), 1)
    if role == "own":
        return jnp.zeros((rows, LANES), BF16)
    offset = OFFSETS[role]
    place = offset + 2 if offset < 0 else offset + 1
    place = place + odd * (3 - 2 * place)
    return jnp.where(lane == place, 1.0, 0.0).astype(BF16)


def attend_kernel(roles, layer, head_dim, me_ref, *refs):
    odd = parity(me_ref)
    blocks, refs = refs[: len(roles)], refs[len(roles) :]
    gate_ref, w_key_ref, w_value_ref, refs = refs[0], refs[1], refs[2], refs[3:]
    first, last = roles[0] == "own", roles[-1] == "far"
    rows, width = blocks[0].shape
    if first:
        w_query_ref, query_ref, acc_ref, norm_ref, top_ref = refs
        query = dot(blocks[0][...], w_query_ref[layer]) * (head_dim**-0.5 * LOG2E)
        query = query.astype(BF16)
        query_ref[...] = query
    elif last:
        (query_in, acc_in, norm_in, top_in, state_in, w_out_ref, mlp_gain_ref, w_up_ref, w_down_ref,
         next_gain_ref, state_ref, normed_ref) = refs
        query = query_in[...]
    else:
        query_in, acc_in, norm_in, top_in, acc_ref, norm_ref, top_ref = refs
        query = query_in[...]
    near = jnp.concatenate([block[...] for block in blocks], axis=0)
    keys = dot(near, w_key_ref[layer]).astype(BF16)
    values = dot(near, w_value_ref[layer]).astype(BF16)
    gates = jnp.concatenate([key_gate(role, odd, rows) for role in roles], axis=0)
    ones = jnp.ones(gates.shape, BF16)
    gate = gate_ref[...]
    low = lax.broadcasted_iota(jnp.int32, (rows, LANES), 1) < head_dim
    pieces = []
    for index in range(width // LANES):
        lanes = slice(index * LANES, (index + 1) * LANES)
        part = query[:, lanes]
        zero = jnp.zeros_like(part)
        queries = jnp.concatenate(
            [
                jnp.concatenate([jnp.where(low, part, zero), gate], axis=1),
                jnp.concatenate([jnp.where(low, zero, part), gate], axis=1),
            ],
            axis=0,
        )
        scores = dot_t(queries, jnp.concatenate([keys[:, lanes], gates], axis=1))
        top = jnp.broadcast_to(jnp.max(scores, axis=1, keepdims=True), (2 * rows, LANES))
        if not first:
            before = top_in[index]
            top = jnp.maximum(top, before)
            fade = jnp.exp2(before - top)
            fade = jnp.where(low, fade[:rows], fade[rows:])
        spread_top = jnp.concatenate([top] * (scores.shape[1] // LANES), axis=1)
        weights = jnp.exp2(scores - spread_top).astype(BF16)
        sums = dot(weights, jnp.concatenate([values[:, lanes], ones], axis=1))
        acc = jnp.where(low, sums[:rows, :LANES], sums[rows:, :LANES])
        norm = jnp.where(low, sums[:rows, LANES:], sums[rows:, LANES:])
        if not first:
            acc = acc_in[:, lanes] * fade + acc
            norm = norm_in[:, lanes] * fade + norm
        if last:
            pieces.append((acc / norm).astype(BF16))
        else:
            acc_ref[:, lanes] = acc
            norm_ref[:, lanes] = norm
            top_ref[index] = top
    if not last:
        return
    state = state_in[...] + dot(jnp.concatenate(pieces, axis=1), w_out_ref[layer])
    normed = rms(state, mlp_gain_ref[layer : layer + 1, :].astype(F32)).astype(BF16)
    up_hidden = silu(dot(normed, w_up_ref[layer])).astype(BF16)
    state = state + dot(up_hidden, w_down_ref[layer])
    gain_row = layer + 1 if layer + 1 < LAYERS else 0
    state_ref[...] = state
    normed_ref[...] = rms(state, next_gain_ref[gain_row : gain_row + 1, :].astype(F32)).astype(BF16)


def pick_rows(ids, roles, odd, decoded):
    id_rows = ids.shape[0] // 2
    mesh_rows = decoded.shape[0] // len(roles)
    node, step = ids[:id_rows].astype(F32), ids[id_rows:].astype(F32)
    code = jnp.full(node.shape, -1.0, F32)
    for place, role in enumerate(roles):
        wanted = jnp.asarray(offset_of(role, odd), jnp.int32).astype(F32)
        code = jnp.where(step == wanted, node + float(place * mesh_rows), code)
    code = jnp.transpose(code)
    nodes = lax.broadcasted_iota(jnp.int32, (LANES, decoded.shape[0]), 1).astype(F32)
    hits = [jnp.where(nodes == code[:, row : row + 1], 1.0, 0.0).astype(BF16) for row in range(id_rows)]
    return dot(jnp.concatenate(hits, axis=0), decoded)


def decode_mid_kernel(roles, me_ref, ids_ref, own_ref, pair_ref, near_ref, wide_ref, rows_ref):
    decoded = jnp.concatenate([own_ref[...], pair_ref[...], near_ref[...], wide_ref[...]], axis=0)
    rows_ref[...] = pick_rows(ids_ref[...], roles, parity(me_ref), decoded).astype(BF16)


def decode_last_kernel(me_ref, ids_ref, far_ref, rows_ref, feat_ref, w_dec_ref, w_head_ref, w_final_ref, out_ref):
    rows = pick_rows(ids_ref[...], ("far",), parity(me_ref), far_ref[...]).astype(BF16) + rows_ref[...]
    mix = (feat_ref[...].astype(F32) + dot(rows, w_dec_ref[...])).astype(BF16)
    head_rows = silu(dot(mix, w_head_ref[...])).astype(BF16)
    out_ref[...] = dot(head_rows, w_final_ref[...]).astype(BF16)


def call(name, kernel, outs, flops):
    def run(*operands):
        specs = [pl.BlockSpec(memory_space=pltpu.SMEM)]
        specs += [pl.BlockSpec(memory_space=pltpu.VMEM) for _ in operands[1:]]
        size = sum(o.size * o.dtype.itemsize for o in operands) + sum(
            int(np.prod(o.shape)) * o.dtype.itemsize for o in outs
        )
        return pl.pallas_call(
            kernel,
            out_shape=outs,
            in_specs=specs,
            out_specs=[pl.BlockSpec(memory_space=pltpu.VMEM) for _ in outs],
            cost_estimate=pl.CostEstimate(flops=flops, bytes_accessed=size, transcendentals=0),
            compiler_params=pltpu.CompilerParams(vmem_limit_bytes=KERNEL_VMEM),
            name=name,
        )(*operands)

    return run


def shape(*sizes, dtype=F32):
    return jax.ShapeDtypeStruct(sizes, dtype)


def body(
    grid_in, dest_block, dest_node, neighbour_mask, mesh_embed, w_in, in_bias, w_grid, w_enc, attn_gain, w_query,
    w_key, w_value, w_out, mlp_gain, w_up, w_down, dec_gain, w_dec, w_head, w_final,
):
    block_count = lax.axis_size("block")
    me = lax.axis_index("block").astype(jnp.int32).reshape(1)
    grid_rows, channels = grid_in.shape
    mesh_rows, width = mesh_embed.shape
    out_width = w_final.shape[1]
    head_dim = width // HEADS
    id_rows = grid_rows // LANES
    bias = in_bias.reshape(1, -1)
    decode_gain = dec_gain.reshape(1, -1)

    packed, ids = call(
        "pack",
        functools.partial(pack_kernel, block_count),
        [shape(grid_rows + 2 * id_rows, channels, dtype=BF16), shape(2 * id_rows, channels, dtype=BF16)],
        grid_rows * channels,
    )(me, grid_in, dest_block.reshape(id_rows, LANES), dest_node.reshape(id_rows, LANES))
    pair, near, wide, far = spread(packed)
    sums = [shape(mesh_rows, width), shape(mesh_rows, LANES)]
    block_flops = 2 * grid_rows * width * (channels + mesh_rows)

    def encode(roles, outs):
        return call(
            "encode_" + roles[0], functools.partial(encode_kernel, roles, grid_rows), outs, len(roles) * block_flops
        )

    total, count, feat, gate = encode(
        ("own", "pair"), sums + [shape(grid_rows, width, dtype=BF16), shape(mesh_rows, LANES, dtype=BF16)]
    )(me, packed, pair, w_in, bias, w_grid, neighbour_mask.T)
    total, count = encode(("near", "wide"), sums)(me, near, wide, w_in, bias, total, count)
    states = [shape(mesh_rows, width), shape(mesh_rows, width, dtype=BF16)]
    state, normed = encode(("far",), states)(
        me, far, w_in, bias, total, count, w_grid, w_enc, mesh_embed, attn_gain
    )
    carries = [shape(mesh_rows, width), shape(mesh_rows, width), shape(width // LANES, 2 * mesh_rows, LANES)]
    attend_flops = 4 * mesh_rows * width * (width + mesh_rows)
    for layer in range(LAYERS):

        def attend(roles, outs):
            return call(
                "attend_" + roles[0],
                functools.partial(attend_kernel, roles, layer, head_dim),
                outs,
                len(roles) * attend_flops,
            )

        pair, near, wide, far = spread(normed)
        query, *carry = attend(("own", "pair"), [shape(mesh_rows, width, dtype=BF16)] + carries)(
            me, normed, pair, gate, w_key, w_value, w_query
        )
        carry = attend(("near", "wide"), carries)(me, near, wide, gate, w_key, w_value, query, *carry)
        state, normed = attend(("far",), states)(
            me, far, gate, w_key, w_value, query, *carry, state, w_out, mlp_gain, w_up, w_down,
            attn_gain if layer + 1 < LAYERS else decode_gain,
        )
    pair, near, wide, far = spread(normed)
    (rows,) = call(
        "decode_mid",
        functools.partial(decode_mid_kernel, ("own", "pair", "near", "wide")),
        [shape(grid_rows, width, dtype=BF16)],
        2 * grid_rows * width * 4 * mesh_rows,
    )(me, ids, normed, pair, near, wide)
    (grid_out,) = call(
        "decode_last",
        decode_last_kernel,
        [shape(grid_rows, out_width, dtype=BF16)],
        2 * grid_rows * width * 3 * width,
    )(me, ids, far, rows, feat, w_dec, w_head, w_final)
    return grid_out


def solution(mesh):
    split = P(("member", "block"), None)
    placed = (split, split, P(("member", "block")), split, split) + (P(),) * 16
    return jax.shard_map(body, mesh=mesh, in_specs=placed, out_specs=split, check_vma=False)
```

time: 125 us -> 85.6 us (0.68)
  Pallas kernels: 62.8 us -> 24 us
  waiting for transfers between devices: 17.8 us -> 39.8 us
  local copies, waits for them, and re-layouts: 16.3 us -> 3.46 us
  starting transfers between devices: 24.4 us -> 17.9 us
  other arithmetic: 3.62 us -> 0 us
    pallas_call x9 -> x12, Pallas kernels: 62.8 us -> 24 us  [run(): pl.pallas_call(kernel, out_shape=outs, in_specs=specs, out_specs=[pl.Bloc...]
    ppermute x16, waiting for transfers between devices: 17.8 us -> 39.8 us  [send(): return lax.ppermute(value, 'block', pairs)]
    ppermute x16, starting transfers between devices: 24.4 us -> 17.9 us  [send(): return lax.ppermute(value, 'block', pairs)]
    squeeze x4 -> x0, local copies, waits for them, and re-layouts: 6.52 us -> none  [the longest x1 3.04 us: body(): w_query[layer]]
    unnamed x53 -> x44, local copies, waits for them, and re-layouts: 7.29 us -> 3.45 us
    concatenate x2 -> x0, other arithmetic: 1.56 us -> none  [the longest x1 0.97 us: body(): packed = jnp.concatenate([grid_in, ids], axis=0)]
  transfers between devices with their start and end apart: 16 -> 16, of which waited for: 6 -> 9; matrix products, arithmetic and copies ran while one was open for 9% -> 0% of each run, Pallas kernels for 31% -> 17%
where the time goes in v2:
time: 85.6 us; the launch traced here: 85.4 us
  waiting for transfers between devices  39.8 us (46%)
  Pallas kernels  24 us (28%)
  starting transfers between devices  17.9 us (21%)
  local copies, waits for them, and re-layouts  3.46 us (4%)
    ppermute x16, waiting for transfers between devices, send(): return lax.ppermute(value, 'block', pairs)  39.8 us
    pallas_call x12, Pallas kernels, run(): pl.pallas_call(kernel, out_shape=outs, in_specs=specs, out_specs=[pl.Bloc...  24 us
    ppermute x16, starting transfers between devices, send(): return lax.ppermute(value, 'block', pairs)  17.9 us
    unnamed x44, local copies, waits for them, and re-layouts  3.45 us
  transfers between devices with their start and end apart: 16, of which 9 were waited for; matrix products, arithmetic and copies ran while one was open for 0% of the time, Pallas kernels for 17%

profile of v2, /device:TPU:0, one launch (start us, length us, event | category | flops | bytes accessed | tf_op | source)
XLA Modules:
  0.0 85.4 jit_solution(9149681507565389860)
XLA Ops:
  0.0 0.7 copy-done.15
  0.7 0.0 copy-done.14
  0.7 0.9 %copy-done.9 = bf16[1024,128]{1,0:T(8,128)(2,1)S(1)} copy-done((bf16[1024,128]{1,0:T(8,128)(2,1)S(1)}, bf16[1024,128]{1,0:T(8,128)(2,1)}, u32[]{:S(2)}) %copy-start.9) | copy-done | bytes 262168
  1.7 0.0 copy-start.19
  1.7 5.5 %collective-permute-start.1 = (bf16[1040,128]{1,0:T(8,128)(2,1)S(1)}, bf16[1040,128]{1,0:T(8,128)(2,1)S(1)}, u32[]{:S(2)}, u32[]{:S(2)}) collective-permute-start(bf16[1040,128]{1,0:T(8,128)(2,1)S(1)} %get-tuple-element.33.refs_0_), channel_id=1, source_target_pairs={{0,15},{1,2},{2,1},{3,4},{4,3},{5,6},{6,5},{7,8},{8,7},{9,10},{10,... | collective-permute-start | bytes 798728 | tf_op jit(solution)/shard_map/ppermute | solution.py:30
  7.2 0.0 collective-permute-start.3
  7.2 4.2 %collective-permute-done.1.refs_0_ = bf16[1040,128]{1,0:T(8,128)(2,1)S(1)} collective-permute-done((bf16[1040,128]{1,0:T(8,128)(2,1)S(1)}, bf16[1040,128]{1,0:T(8,128)(2,1)S(1)}, u32[]{:S(2)}, u32[]{:S(2)}) %collective-permute-start.1) | collective-permute-done | bytes 266272 | tf_op jit(solution)/shard_map/ppermute | solution.py:30
  11.4 0.4 collective-permute-start.2
  11.8 1.6 %collective-permute-start = (bf16[1040,128]{1,0:T(8,128)(2,1)S(1)}, bf16[1040,128]{1,0:T(8,128)(2,1)S(1)}, u32[]{:S(2)}, u32[]{:S(2)}) collective-permute-start(bf16[1040,128]{1,0:T(8,128)(2,1)S(1)} %get-tuple-element.33.refs_0_), channel_id=1, source_target_pairs={{0,2},{1,15},{2,4},{3,1},{4,6},{5,3},{6,8},{7,5},{8,10},{9,7},{10,... | collective-permute-start | bytes 798728 | tf_op jit(solution)/shard_map/ppermute | solution.py:30
  13.5 0.0 collective-permute-done.3.refs_1_
  13.5 0.0 copy-done.11
  13.5 0.0 copy-done.19
  13.5 0.0 copy-start.6
  13.5 1.0 %copy-done.6 = bf16[512,512]{1,0:T(8,128)(2,1)S(1)} copy-done((bf16[512,512]{1,0:T(8,128)(2,1)S(1)}, bf16[512,512]{1,0:T(8,128)(2,1)}, u32[]{:S(2)}) %copy-start.6) | copy-done | bytes 524312
  14.5 2.2 %encode_own.1 = (f32[256,512]{1,0:T(8,128)S(1)}, f32[256,128]{1,0:T(8,128)S(1)}, bf16[1024,512]{1,0:T(8,128)(2,1)S(1)}, bf16[256,128]{1,0:T(8,128)(2,1)S(1)}) custom-call(s32[1]{0:T(128)} %bitcast.me_ref, bf16[1040,128]{1,0:T(8,128)(2,1)S(1)} %get-tuple-element.33.refs_0_, bf16[1040,128]{1,0:T(8,128)(2,1)S(1)} %collective-permute-done.3.refs_1_, ...), custom_call_target="tpu_custom_call" | custom-call | flops 805306368 | bytes 2962436 | tf_op jit(solution)/shard_map/encode_own/pallas_call | solution.py:242
  16.8 0.0 collective-permute-done.2.refs_1_
  16.8 0.0 copy-start.7
  16.8 0.0 copy-start.8
  16.8 0.0 copy-start.10
  16.8 0.0 copy-start.2
  16.8 1.8 %encode_near.1 = (f32[256,512]{1,0:T(8,128)S(1)}, f32[256,128]{1,0:T(8,128)S(1)}) custom-call(s32[1]{0:T(128)} %bitcast.me_ref, bf16[1040,128]{1,0:T(8,128)(2,1)S(1)} %collective-permute-done.1.refs_0_, bf16[1040,128]{1,0:T(8,128)(2,1)S(1)} %collective-permute-done.2.refs_1_, bf16[128,512]{1,0:T(8,128)(2,1)S(1)} %copy-done.11, ...), custom_call_target="tpu_custom_call" | custom-call | flops 805306368 | bytes 1975300 | tf_op jit(solution)/shard_map/encode_near/pallas_call | solution.py:242
  18.6 0.0 copy-start.12
  18.6 2.3 %collective-permute-done.refs_0_ = bf16[1040,128]{1,0:T(8,128)(2,1)S(1)} collective-permute-done((bf16[1040,128]{1,0:T(8,128)(2,1)S(1)}, bf16[1040,128]{1,0:T(8,128)(2,1)S(1)}, u32[]{:S(2)}, u32[]{:S(2)}) %collective-permute-start) | collective-permute-done | bytes 266272 | tf_op jit(solution)/shard_map/ppermute | solution.py:30
  20.9 0.0 copy-done.7
  21.0 0.0 copy-start
  21.0 0.0 copy-start.1
  21.0 1.4 %encode_far.1 = (f32[256,512]{1,0:T(8,128)S(1)}, bf16[256,512]{1,0:T(8,128)(2,1)S(1)}) custom-call(s32[1]{0:T(128)} %bitcast.me_ref, bf16[1040,128]{1,0:T(8,128)(2,1)S(1)} %collective-permute-done.refs_0_, bf16[128,512]{1,0:T(8,128)(2,1)S(1)} %copy-done.11, bf16[1,512]{1,0:T(2,128)(2,1)S(1)} %reshape.18.refs_3_.refs_2_, ...), custom_call_target="tpu_custom_call" | custom-call | flops 402653184 | bytes 3152900 | tf_op jit(solution)/shard_map/encode_far/pallas_call | solution.py:242
  22.4 3.8 %collective-permute-start.6 = (bf16[256,512]{1,0:T(8,128)(2,1)S(1)}, bf16[256,512]{1,0:T(8,128)(2,1)S(1)}, u32[]{:S(2)}, u32[]{:S(2)}) collective-permute-start(bf16[256,512]{1,0:T(8,128)(2,1)S(1)} %get-tuple-element.38.refs_0_), channel_id=1, source_target_pairs={{0,15},{1,2},{2,1},{3,4},{4,3},{5,6},{6,5},{7,8},{8,7},{9,10},{10,... | collective-permute-start | bytes 786440 | tf_op jit(solution)/shard_map/ppermute | solution.py:30
  26.2 0.0 collective-permute-start.5
  26.2 4.9 %collective-permute-done.6.refs_0_ = bf16[256,512]{1,0:T(8,128)(2,1)S(1)} collective-permute-done((bf16[256,512]{1,0:T(8,128)(2,1)S(1)}, bf16[256,512]{1,0:T(8,128)(2,1)S(1)}, u32[]{:S(2)}, u32[]{:S(2)}) %collective-permute-start.6) | collective-permute-done | bytes 262176 | tf_op jit(solution)/shard_map/ppermute | solution.py:30
  31.1 1.6 %collective-permute-start.7 = (bf16[256,512]{1,0:T(8,128)(2,1)S(1)}, bf16[256,512]{1,0:T(8,128)(2,1)S(1)}, u32[]{:S(2)}, u32[]{:S(2)}) collective-permute-start(bf16[256,512]{1,0:T(8,128)(2,1)S(1)} %collective-permute-done.6.refs_0_), channel_id=1, source_target_pairs={{0,1},{1,0},{2,3},{3,2},{4,5},{5,4},{6,7},{7,6},{8,9},{9,8},{10,11... | collective-permute-start | bytes 786440 | tf_op jit(solution)/shard_map/ppermute | solution.py:30
  32.7 0.0 collective-permute-start.4
  32.7 0.0 collective-permute-done.5.refs_1_
  32.7 2.3 %attend_own.2 = (bf16[256,512]{1,0:T(8,128)(2,1)S(1)}, f32[256,512]{1,0:T(8,128)S(1)}, f32[256,512]{1,0:T(8,128)S(1)}, f32[4,512,128]{2,1,0:T(8,128)S(1)}) custom-call(s32[1]{0:T(128)} %bitcast.me_ref, bf16[256,512]{1,0:T(8,128)(2,1)S(1)} %get-tuple-element.38.refs_0_, bf16[256,512]{1,0:T(8,128)(2,1)S(1)} %collective-permute-done.5.refs_1_, ...), custom_call_target="tpu_custom_call" | custom-call | flops 805306368 | bytes 6094852 | tf_op jit(solution)/shard_map/attend_own/pallas_call | solution.py:242
  35.1 0.0 collective-permute-done.7.refs_1_
  35.1 0.0 copy-start.3
  35.1 0.0 copy-start.4
  35.1 0.0 copy-start.5
  35.1 2.4 %attend_near.2 = (f32[256,512]{1,0:T(8,128)S(1)}, f32[256,512]{1,0:T(8,128)S(1)}, f32[4,512,128]{2,1,0:T(8,128)S(1)}) custom-call(s32[1]{0:T(128)} %bitcast.me_ref, bf16[256,512]{1,0:T(8,128)(2,1)S(1)} %collective-permute-done.6.refs_0_, bf16[256,512]{1,0:T(8,128)(2,1)S(1)} %collective-permute-done.7.refs_1_, ...), custom_call_target="tpu_custom_call" | custom-call | flops 805306368 | bytes 7143428 | tf_op jit(solution)/shard_map/attend_near/pallas_call | solution.py:242
  37.5 4.3 %collective-permute-done.4.refs_0_ = bf16[256,512]{1,0:T(8,128)(2,1)S(1)} collective-permute-done((bf16[256,512]{1,0:T(8,128)(2,1)S(1)}, bf16[256,512]{1,0:T(8,128)(2,1)S(1)}, u32[]{:S(2)}, u32[]{:S(2)}) %collective-permute-start.4) | collective-permute-done | bytes 262176 | tf_op jit(solution)/shard_map/ppermute | solution.py:30
  41.8 0.7 copy-done.13
  42.5 2.1 %attend_far.2 = (f32[256,512]{1,0:T(8,128)S(1)}, bf16[256,512]{1,0:T(8,128)(2,1)S(1)}) custom-call(s32[1]{0:T(128)} %bitcast.me_ref, bf16[256,512]{1,0:T(8,128)(2,1)S(1)} %collective-permute-done.4.refs_0_, bf16[256,128]{1,0:T(8,128)(2,1)S(1)} %get-tuple-element.39.refs_2_.refs_1_, bf16[2,512,512]{2,1,0:T(8,128)(2,1)S(1)} %copy-done, ...), custom_call_target="tpu_custom_call" | custom-call | flops 402653184 | bytes 9244676 | tf_op jit(solution)/shard_map/attend_far/pallas_call | solution.py:242
  44.6 0.0 copy-start.21
  44.6 2.4 %collective-permute-start.10 = (bf16[256,512]{1,0:T(8,128)(2,1)S(1)}, bf16[256,512]{1,0:T(8,128)(2,1)S(1)}, u32[]{:S(2)}, u32[]{:S(2)}) collective-permute-start(bf16[256,512]{1,0:T(8,128)(2,1)S(1)} %get-tuple-element.48.refs_0_), channel_id=1, source_target_pairs={{0,15},{1,2},{2,1},{3,4},{4,3},{5,6},{6,5},{7,8},{8,7},{9,10},{10,... | collective-permute-start | bytes 786440 | tf_op jit(solution)/shard_map/ppermute | solution.py:30
  47.0 0.0 collective-permute-start.9
  47.0 6.2 %collective-permute-done.10.refs_0_ = bf16[256,512]{1,0:T(8,128)(2,1)S(1)} collective-permute-done((bf16[256,512]{1,0:T(8,128)(2,1)S(1)}, bf16[256,512]{1,0:T(8,128)(2,1)S(1)}, u32[]{:S(2)}, u32[]{:S(2)}) %collective-permute-start.10) | collective-permute-done | bytes 262176 | tf_op jit(solution)/shard_map/ppermute | solution.py:30
  53.2 0.0 collective-permute-start.11
  53.2 0.0 collective-permute-start.8
  53.2 0.0 collective-permute-done.9.refs_1_
  53.2 2.3 %attend_own.3 = (bf16[256,512]{1,0:T(8,128)(2,1)S(1)}, f32[256,512]{1,0:T(8,128)S(1)}, f32[256,512]{1,0:T(8,128)S(1)}, f32[4,512,128]{2,1,0:T(8,128)S(1)}) custom-call(s32[1]{0:T(128)} %bitcast.me_ref, bf16[256,512]{1,0:T(8,128)(2,1)S(1)} %get-tuple-element.48.refs_0_, bf16[256,512]{1,0:T(8,128)(2,1)S(1)} %collective-permute-done.9.refs_1_, ...), custom_call_target="tpu_custom_call" | custom-call | flops 805306368 | bytes 6094852 | tf_op jit(solution)/shard_map/attend_own/pallas_call | solution.py:242
  55.6 0.0 collective-permute-done.11.refs_1_
  55.6 2.4 %attend_near.3 = (f32[256,512]{1,0:T(8,128)S(1)}, f32[256,512]{1,0:T(8,128)S(1)}, f32[4,512,128]{2,1,0:T(8,128)S(1)}) custom-call(s32[1]{0:T(128)} %bitcast.me_ref, bf16[256,512]{1,0:T(8,128)(2,1)S(1)} %collective-permute-done.10.refs_0_, bf16[256,512]{1,0:T(8,128)(2,1)S(1)} %collective-permute-done.11.refs_1_, ...), custom_call_target="tpu_custom_call" | custom-call | flops 805306368 | bytes 7143428 | tf_op jit(solution)/shard_map/attend_near/pallas_call | solution.py:242
  58.0 4.3 %collective-permute-done.8.refs_0_ = bf16[256,512]{1,0:T(8,128)(2,1)S(1)} collective-permute-done((bf16[256,512]{1,0:T(8,128)(2,1)S(1)}, bf16[256,512]{1,0:T(8,128)(2,1)S(1)}, u32[]{:S(2)}, u32[]{:S(2)}) %collective-permute-start.8) | collective-permute-done | bytes 262176 | tf_op jit(solution)/shard_map/ppermute | solution.py:30
  62.2 2.8 %attend_far.3 = (f32[256,512]{1,0:T(8,128)}, bf16[256,512]{1,0:T(8,128)(2,1)S(1)}) custom-call(s32[1]{0:T(128)} %bitcast.me_ref, bf16[256,512]{1,0:T(8,128)(2,1)S(1)} %collective-permute-done.8.refs_0_, bf16[256,128]{1,0:T(8,128)(2,1)S(1)} %get-tuple-element.39.refs_2_.refs_1_, bf16[2,512,512]{2,1,0:T(8,128)(2,1)S(1)} %copy-done, ...), custom_call_target="tpu_custom_call" | custom-call | flops 402653184 | bytes 9243652 | tf_op jit(solution)/shard_map/attend_far/pallas_call | solution.py:242
  65.1 2.5 %collective-permute-start.14 = (bf16[256,512]{1,0:T(8,128)(2,1)S(1)}, bf16[256,512]{1,0:T(8,128)(2,1)S(1)}, u32[]{:S(2)}, u32[]{:S(2)}) collective-permute-start(bf16[256,512]{1,0:T(8,128)(2,1)S(1)} %get-tuple-element.57.own_ref), channel_id=1, source_target_pairs={{0,15},{1,2},{2,1},{3,4},{4,3},{5,6},{6,5},{7,8},{8,7},{9,10},{10,... | collective-permute-start | bytes 786440 | tf_op jit(solution)/shard_map/ppermute | solution.py:30
  67.6 0.0 collective-permute-start.13
  67.6 6.0 %collective-permute-done.14.near_ref = bf16[256,512]{1,0:T(8,128)(2,1)S(1)} collective-permute-done((bf16[256,512]{1,0:T(8,128)(2,1)S(1)}, bf16[256,512]{1,0:T(8,128)(2,1)S(1)}, u32[]{:S(2)}, u32[]{:S(2)}) %collective-permute-start.14) | collective-permute-done | bytes 262176 | tf_op jit(solution)/shard_map/ppermute | solution.py:30
  73.6 0.0 collective-permute-start.15
  73.6 0.0 collective-permute-start.12
  73.6 0.0 collective-permute-done.13.pair_ref
  73.6 1.5 %collective-permute-done.15.wide_ref = bf16[256,512]{1,0:T(8,128)(2,1)S(1)} collective-permute-done((bf16[256,512]{1,0:T(8,128)(2,1)S(1)}, bf16[256,512]{1,0:T(8,128)(2,1)S(1)}, u32[]{:S(2)}, u32[]{:S(2)}) %collective-permute-start.15) | collective-permute-done | bytes 262176 | tf_op jit(solution)/shard_map/ppermute | solution.py:30
  75.1 1.4 %decode_mid.1.rows_ref = bf16[1024,512]{1,0:T(8,128)(2,1)S(1)} custom-call(s32[1]{0:T(128)} %bitcast.me_ref, bf16[16,128]{1,0:T(8,128)(2,1)S(1)} %get-tuple-element.32.ids_ref, bf16[256,512]{1,0:T(8,128)(2,1)S(1)} %get-tuple-element.57.own_ref, bf16[256,512]{1,0:T(8,128)(2,1)S(1)} %collective-permute-done.13.pair_ref, ...), custom_call_target="tpu_custom_call" | custom-call | flops 1073741824 | bytes 2101252 | tf_op jit(solution)/shard_map/decode_mid/pallas_call | solution.py:242
  76.5 6.2 %collective-permute-done.12.far_ref = bf16[256,512]{1,0:T(8,128)(2,1)S(1)} collective-permute-done((bf16[256,512]{1,0:T(8,128)(2,1)S(1)}, bf16[256,512]{1,0:T(8,128)(2,1)S(1)}, u32[]{:S(2)}, u32[]{:S(2)}) %collective-permute-start.12) | collective-permute-done | bytes 262176 | tf_op jit(solution)/shard_map/ppermute | solution.py:30
  82.6 2.7 %decode_last.1 = bf16[1024,128]{1,0:T(8,128)(2,1)} custom-call(s32[1]{0:T(128)} %bitcast.me_ref, bf16[16,128]{1,0:T(8,128)(2,1)S(1)} %get-tuple-element.32.ids_ref, bf16[256,512]{1,0:T(8,128)(2,1)S(1)} %collective-permute-done.12.far_ref, bf16[1024,512]{1,0:T(8,128)(2,1)S(1)} %decode_mid.1.rows_ref, bf16[1024,512]{1,0:T(8,128)(2,1)S(1)} %get-tuple-element.58.feat_ref, ...), custom_call_target="tpu_custom_call" | custom-call | flops 1610612736 | bytes 3805188 | tf_op jit(solution)/shard_map/decode_last/pallas_call | solution.py:242
  (26 shorter events, 0.1 us)
Async XLA Ops:
  0.0 0.7 copy-start.15
  0.0 0.7 copy-start.14
  0.7 0.9 %copy-start.9 = (bf16[1024,128]{1,0:T(8,128)(2,1)S(1)}, bf16[1024,128]{1,0:T(8,128)(2,1)}, u32[]{:S(2)}) copy-start(bf16[1024,128]{1,0:T(8,128)(2,1)} %grid_ref.1) | copy-start | bytes 786436
  1.7 11.8 %copy-start.20 = (bf16[512]{0:T(512)(128)(2,1)S(1)}, bf16[512]{0:T(512)(128)(2,1)}, u32[]{:S(2)}) copy-start(bf16[512]{0:T(512)(128)(2,1)} %param.27) | copy-start | bytes 3076
  1.7 11.8 %copy-start.11 = (bf16[128,512]{1,0:T(8,128)(2,1)S(1)}, bf16[128,512]{1,0:T(8,128)(2,1)}, u32[]{:S(2)}) copy-start(bf16[128,512]{1,0:T(8,128)(2,1)} %refs_1_.1) | copy-start | bytes 393220
  1.7 11.8 %copy-start.19 = (s32[256,4]{0,1:T(4,128)S(1)}, s32[256,4]{0,1:T(4,128)}, u32[]{:S(2)}) copy-start(s32[256,4]{0,1:T(4,128)} %param.24) | copy-start | bytes 12292
  1.7 9.7 %collective-permute-start.1 = (bf16[1040,128]{1,0:T(8,128)(2,1)S(1)}, bf16[1040,128]{1,0:T(8,128)(2,1)S(1)}, u32[]{:S(2)}, u32[]{:S(2)}) collective-permute-start(bf16[1040,128]{1,0:T(8,128)(2,1)S(1)} %get-tuple-element.33.refs_0_), channel_id=1, source_target_pairs={{0,15},{1,2},{2,1},{3,4},{4,3},{5,6},{6,5},{7,8},{8,7},{9,10},{10,... | collective-permute-start | bytes 798728 | tf_op jit(solution)/shard_map/ppermute | solution.py:30
  7.2 6.2 %collective-permute-start.3 = (bf16[1040,128]{1,0:T(8,128)(2,1)S(1)}, bf16[1040,128]{1,0:T(8,128)(2,1)S(1)}, u32[]{:S(2)}, u32[]{:S(2)}) collective-permute-start(bf16[1040,128]{1,0:T(8,128)(2,1)S(1)} %get-tuple-element.33.refs_0_), channel_id=1, source_target_pairs={{0,1},{1,0},{2,3},{3,2},{4,5},{5,4},{6,7},{7,6},{8,9},{9,8},{10,11... | collective-permute-start | bytes 798728 | tf_op jit(solution)/shard_map/ppermute | solution.py:30
  11.4 5.3 %collective-permute-start.2 = (bf16[1040,128]{1,0:T(8,128)(2,1)S(1)}, bf16[1040,128]{1,0:T(8,128)(2,1)S(1)}, u32[]{:S(2)}, u32[]{:S(2)}) collective-permute-start(bf16[1040,128]{1,0:T(8,128)(2,1)S(1)} %collective-permute-done.1.refs_0_), channel_id=1, source_target_pairs={{0,1},{1,0},{2,3},{3,2},{4,5},{5,4},{6,7},{7,6},{8,9},{9,8},{10,11... | collective-permute-start | bytes 798728 | tf_op jit(solution)/shard_map/ppermute | solution.py:30
  11.8 9.1 %collective-permute-start = (bf16[1040,128]{1,0:T(8,128)(2,1)S(1)}, bf16[1040,128]{1,0:T(8,128)(2,1)S(1)}, u32[]{:S(2)}, u32[]{:S(2)}) collective-permute-start(bf16[1040,128]{1,0:T(8,128)(2,1)S(1)} %get-tuple-element.33.refs_0_), channel_id=1, source_target_pairs={{0,2},{1,15},{2,4},{3,1},{4,6},{5,3},{6,8},{7,5},{8,10},{9,7},{10,... | collective-permute-start | bytes 798728 | tf_op jit(solution)/shard_map/ppermute | solution.py:30
  13.5 1.0 %copy-start.6 = (bf16[512,512]{1,0:T(8,128)(2,1)S(1)}, bf16[512,512]{1,0:T(8,128)(2,1)}, u32[]{:S(2)}) copy-start(bf16[512,512]{1,0:T(8,128)(2,1)} %refs_5_.3) | copy-start | bytes 1572868
  16.8 4.2 %copy-start.7 = (bf16[512,512]{1,0:T(8,128)(2,1)S(1)}, bf16[512,512]{1,0:T(8,128)(2,1)}, u32[]{:S(2)}) copy-start(bf16[512,512]{1,0:T(8,128)(2,1)} %refs_5_.3) | copy-start | bytes 1572868
  16.8 4.2 %copy-start.8 = (bf16[512,512]{1,0:T(8,128)(2,1)S(1)}, bf16[512,512]{1,0:T(8,128)(2,1)}, u32[]{:S(2)}) copy-start(bf16[512,512]{1,0:T(8,128)(2,1)} %refs_6_.1) | copy-start | bytes 1572868
  16.8 4.1 %copy-start.10 = (bf16[256,512]{1,0:T(8,128)(2,1)S(1)}, bf16[256,512]{1,0:T(8,128)(2,1)}, u32[]{:S(2)}) copy-start(bf16[256,512]{1,0:T(8,128)(2,1)} %refs_7_.1) | copy-start | bytes 786436
  16.8 15.9 %copy-start.2 = (bf16[2,512,512]{2,1,0:T(8,128)(2,1)S(1)}, bf16[2,512,512]{2,1,0:T(8,128)(2,1)}, u32[]{:S(2)}) copy-start(bf16[2,512,512]{2,1,0:T(8,128)(2,1)} %refs_5_.5) | copy-start | bytes 3145732
  18.6 2.3 %copy-start.12 = (bf16[2,512]{1,0:T(2,128)(2,1)S(1)}, bf16[2,512]{1,0:T(2,128)(2,1)}, u32[]{:S(2)}) copy-start(bf16[2,512]{1,0:T(2,128)(2,1)} %refs_13_.1) | copy-start | bytes 6148
  21.0 11.8 %copy-start = (bf16[2,512,512]{2,1,0:T(8,128)(2,1)S(1)}, bf16[2,512,512]{2,1,0:T(8,128)(2,1)}, u32[]{:S(2)}) copy-start(bf16[2,512,512]{2,1,0:T(8,128)(2,1)} %refs_2_.7) | copy-start | bytes 3145732
  21.0 11.8 %copy-start.1 = (bf16[2,512,512]{2,1,0:T(8,128)(2,1)S(1)}, bf16[2,512,512]{2,1,0:T(8,128)(2,1)}, u32[]{:S(2)}) copy-start(bf16[2,512,512]{2,1,0:T(8,128)(2,1)} %refs_3_.11) | copy-start | bytes 3145732
  22.4 8.7 %collective-permute-start.6 = (bf16[256,512]{1,0:T(8,128)(2,1)S(1)}, bf16[256,512]{1,0:T(8,128)(2,1)S(1)}, u32[]{:S(2)}, u32[]{:S(2)}) collective-permute-start(bf16[256,512]{1,0:T(8,128)(2,1)S(1)} %get-tuple-element.38.refs_0_), channel_id=1, source_target_pairs={{0,15},{1,2},{2,1},{3,4},{4,3},{5,6},{6,5},{7,8},{8,7},{9,10},{10,... | collective-permute-start | bytes 786440 | tf_op jit(solution)/shard_map/ppermute | solution.py:30
  26.2 6.5 %collective-permute-start.5 = (bf16[256,512]{1,0:T(8,128)(2,1)S(1)}, bf16[256,512]{1,0:T(8,128)(2,1)S(1)}, u32[]{:S(2)}, u32[]{:S(2)}) collective-permute-start(bf16[256,512]{1,0:T(8,128)(2,1)S(1)} %get-tuple-element.38.refs_0_), channel_id=1, source_target_pairs={{0,1},{1,0},{2,3},{3,2},{4,5},{5,4},{6,7},{7,6},{8,9},{9,8},{10,11... | collective-permute-start | bytes 786440 | tf_op jit(solution)/shard_map/ppermute | solution.py:30
  31.1 4.0 %collective-permute-start.7 = (bf16[256,512]{1,0:T(8,128)(2,1)S(1)}, bf16[256,512]{1,0:T(8,128)(2,1)S(1)}, u32[]{:S(2)}, u32[]{:S(2)}) collective-permute-start(bf16[256,512]{1,0:T(8,128)(2,1)S(1)} %collective-permute-done.6.refs_0_), channel_id=1, source_target_pairs={{0,1},{1,0},{2,3},{3,2},{4,5},{5,4},{6,7},{7,6},{8,9},{9,8},{10,11... | collective-permute-start | bytes 786440 | tf_op jit(solution)/shard_map/ppermute | solution.py:30
  32.7 9.1 %collective-permute-start.4 = (bf16[256,512]{1,0:T(8,128)(2,1)S(1)}, bf16[256,512]{1,0:T(8,128)(2,1)S(1)}, u32[]{:S(2)}, u32[]{:S(2)}) collective-permute-start(bf16[256,512]{1,0:T(8,128)(2,1)S(1)} %get-tuple-element.38.refs_0_), channel_id=1, source_target_pairs={{0,2},{1,15},{2,4},{3,1},{4,6},{5,3},{6,8},{7,5},{8,10},{9,7},{10,... | collective-permute-start | bytes 786440 | tf_op jit(solution)/shard_map/ppermute | solution.py:30
  35.1 6.7 %copy-start.3 = (bf16[2,512,512]{2,1,0:T(8,128)(2,1)S(1)}, bf16[2,512,512]{2,1,0:T(8,128)(2,1)}, u32[]{:S(2)}) copy-start(bf16[2,512,512]{2,1,0:T(8,128)(2,1)} %refs_9_.3) | copy-start | bytes 3145732
  35.1 6.7 %copy-start.4 = (bf16[2,512,512]{2,1,0:T(8,128)(2,1)S(1)}, bf16[2,512,512]{2,1,0:T(8,128)(2,1)}, u32[]{:S(2)}) copy-start(bf16[2,512,512]{2,1,0:T(8,128)(2,1)} %refs_11_.3) | copy-start | bytes 3145732
  35.1 6.7 %copy-start.5 = (bf16[2,512,512]{2,1,0:T(8,128)(2,1)S(1)}, bf16[2,512,512]{2,1,0:T(8,128)(2,1)}, u32[]{:S(2)}) copy-start(bf16[2,512,512]{2,1,0:T(8,128)(2,1)} %refs_12_.3) | copy-start | bytes 3145732
  41.8 0.7 copy-start.13
  44.6 8.6 %copy-start.21 = (bf16[512]{0:T(512)(128)(2,1)S(1)}, bf16[512]{0:T(512)(128)(2,1)}, u32[]{:S(2)}) copy-start(bf16[512]{0:T(512)(128)(2,1)} %param.38) | copy-start | bytes 3076
  44.6 8.6 %collective-permute-start.10 = (bf16[256,512]{1,0:T(8,128)(2,1)S(1)}, bf16[256,512]{1,0:T(8,128)(2,1)S(1)}, u32[]{:S(2)}, u32[]{:S(2)}) collective-permute-start(bf16[256,512]{1,0:T(8,128)(2,1)S(1)} %get-tuple-element.48.refs_0_), channel_id=1, source_target_pairs={{0,15},{1,2},{2,1},{3,4},{4,3},{5,6},{6,5},{7,8},{8,7},{9,10},{10,... | collective-permute-start | bytes 786440 | tf_op jit(solution)/shard_map/ppermute | solution.py:30
  47.0 6.2 %collective-permute-start.9 = (bf16[256,512]{1,0:T(8,128)(2,1)S(1)}, bf16[256,512]{1,0:T(8,128)(2,1)S(1)}, u32[]{:S(2)}, u32[]{:S(2)}) collective-permute-start(bf16[256,512]{1,0:T(8,128)(2,1)S(1)} %get-tuple-element.48.refs_0_), channel_id=1, source_target_pairs={{0,1},{1,0},{2,3},{3,2},{4,5},{5,4},{6,7},{7,6},{8,9},{9,8},{10,11... | collective-permute-start | bytes 786440 | tf_op jit(solution)/shard_map/ppermute | solution.py:30
  53.2 2.4 %collective-permute-start.11 = (bf16[256,512]{1,0:T(8,128)(2,1)S(1)}, bf16[256,512]{1,0:T(8,128)(2,1)S(1)}, u32[]{:S(2)}, u32[]{:S(2)}) collective-permute-start(bf16[256,512]{1,0:T(8,128)(2,1)S(1)} %collective-permute-done.10.refs_0_), channel_id=1, source_target_pairs={{0,1},{1,0},{2,3},{3,2},{4,5},{5,4},{6,7},{7,6},{8,9},{9,8},{10,11... | collective-permute-start | bytes 786440 | tf_op jit(solution)/shard_map/ppermute | solution.py:30
  53.2 9.1 %collective-permute-start.8 = (bf16[256,512]{1,0:T(8,128)(2,1)S(1)}, bf16[256,512]{1,0:T(8,128)(2,1)S(1)}, u32[]{:S(2)}, u32[]{:S(2)}) collective-permute-start(bf16[256,512]{1,0:T(8,128)(2,1)S(1)} %get-tuple-element.48.refs_0_), channel_id=1, source_target_pairs={{0,2},{1,15},{2,4},{3,1},{4,6},{5,3},{6,8},{7,5},{8,10},{9,7},{10,... | collective-permute-start | bytes 786440 | tf_op jit(solution)/shard_map/ppermute | solution.py:30
  65.1 8.5 %collective-permute-start.14 = (bf16[256,512]{1,0:T(8,128)(2,1)S(1)}, bf16[256,512]{1,0:T(8,128)(2,1)S(1)}, u32[]{:S(2)}, u32[]{:S(2)}) collective-permute-start(bf16[256,512]{1,0:T(8,128)(2,1)S(1)} %get-tuple-element.57.own_ref), channel_id=1, source_target_pairs={{0,15},{1,2},{2,1},{3,4},{4,3},{5,6},{6,5},{7,8},{8,7},{9,10},{10,... | collective-permute-start | bytes 786440 | tf_op jit(solution)/shard_map/ppermute | solution.py:30
  67.6 6.0 %collective-permute-start.13 = (bf16[256,512]{1,0:T(8,128)(2,1)S(1)}, bf16[256,512]{1,0:T(8,128)(2,1)S(1)}, u32[]{:S(2)}, u32[]{:S(2)}) collective-permute-start(bf16[256,512]{1,0:T(8,128)(2,1)S(1)} %get-tuple-element.57.own_ref), channel_id=1, source_target_pairs={{0,1},{1,0},{2,3},{3,2},{4,5},{5,4},{6,7},{7,6},{8,9},{9,8},{10,11... | collective-permute-start | bytes 786440 | tf_op jit(solution)/shard_map/ppermute | solution.py:30
  73.6 1.5 %collective-permute-start.15 = (bf16[256,512]{1,0:T(8,128)(2,1)S(1)}, bf16[256,512]{1,0:T(8,128)(2,1)S(1)}, u32[]{:S(2)}, u32[]{:S(2)}) collective-permute-start(bf16[256,512]{1,0:T(8,128)(2,1)S(1)} %collective-permute-done.14.near_ref), channel_id=1, source_target_pairs={{0,1},{1,0},{2,3},{3,2},{4,5},{5,4},{6,7},{7,6},{8,9},{9,8},{10,11... | collective-permute-start | bytes 786440 | tf_op jit(solution)/shard_map/ppermute | solution.py:30
  73.6 9.1 %collective-permute-start.12 = (bf16[256,512]{1,0:T(8,128)(2,1)S(1)}, bf16[256,512]{1,0:T(8,128)(2,1)S(1)}, u32[]{:S(2)}, u32[]{:S(2)}) collective-permute-start(bf16[256,512]{1,0:T(8,128)(2,1)S(1)} %get-tuple-element.57.own_ref), channel_id=1, source_target_pairs={{0,2},{1,15},{2,4},{3,1},{4,6},{5,3},{6,8},{7,5},{8,10},{9,7},{10,... | collective-permute-start | bytes 786440 | tf_op jit(solution)/shard_map/ppermute | solution.py:30
  75.1 7.5 %copy-start.16 = (bf16[512,512]{1,0:T(8,128)(2,1)S(1)}, bf16[512,512]{1,0:T(8,128)(2,1)}, u32[]{:S(2)}) copy-start(bf16[512,512]{1,0:T(8,128)(2,1)} %w_dec_ref.1) | copy-start | bytes 1572868
  75.1 7.5 %copy-start.17 = (bf16[512,512]{1,0:T(8,128)(2,1)S(1)}, bf16[512,512]{1,0:T(8,128)(2,1)}, u32[]{:S(2)}) copy-start(bf16[512,512]{1,0:T(8,128)(2,1)} %w_head_ref.1) | copy-start | bytes 1572868
  75.1 7.5 %copy-start.18 = (bf16[512,128]{1,0:T(8,128)(2,1)S(1)}, bf16[512,128]{1,0:T(8,128)(2,1)}, u32[]{:S(2)}) copy-start(bf16[512,128]{1,0:T(8,128)(2,1)} %w_final_ref.1) | copy-start | bytes 393220
